TPU v7x, 512 devices: a whole 4x4x16 slice. The times are simulated.
512 devices in a mesh: lat: 16 (over z_lo, core), lon: 32 (over x, y, z_hi).
Axes of the slice: x: 4, y: 4, z: 16 (z_hi: 2, z_lo: 8; z = z_hi * 8 + z_lo), core: 2. Of those that a mesh axis runs over, the one named last changes fastest.
Arguments:
- student: bfloat16 [2, 64, 1024, 256], P(None, 'lat', 'lon'), may hold values from -6 to 6
- teacher: bfloat16 [2, 64, 1024, 256], P(None, None, ('lon', 'lat')), may hold values from -6 to 6
- dw_weight: float32 [7, 7, 256], replicated, may hold values from -0.875 to 0.875
- norm_gain: float32 [256], replicated, may hold values from 0.1 to 1.9
- w_in: bfloat16 [256, 1024], replicated, may hold values from -0.375 to 0.375
- w_out: bfloat16 [1024, 256], replicated, may hold values from -0.1875 to 0.1875
- layer_scale: float32 [256], replicated, may hold values from 0.3 to 1.5
Outputs:
- grad_student: bfloat16 [2, 64, 1024, 256], P(None, 'lat', 'lon')
- grad_w_in: float32 [256, 1024], replicated
- grad_w_out: float32 [1024, 256], replicated
- grad_dw: float32 [7, 7, 256], replicated
All inputs are finite; a program needn't handle non-finite values.
Results may differ from a plain program's by a relative error of at most 0.0034.
The roundings to bfloat16 on the way count: a program that leaves them out, or rounds other values in their place, can miss the bound.
Values may be sent and summed in bfloat16 or wider, within the bound.
A program may use at most 64 MiB of HBM per device.

v0:
```python
import jax
import jax.numpy as jnp
from jax import lax
from jax.sharding import PartitionSpec as P

slope_coef = 0.7978845608028654
cubic_coef = 0.044715
norm_eps = 1e-06


def with_halo(block, sides, width, periodic):
    for axis, dim in sides:
        count = lax.axis_size(axis)
        forward = [(i, i + 1) for i in range(count - 1)]
        if periodic:
            forward.append((count - 1, 0))
        backward = [(target, source) for source, target in forward]
        low = lax.ppermute(
            lax.slice_in_dim(block, block.shape[dim] - width, None, axis=dim), axis, forward
        )
        high = lax.ppermute(lax.slice_in_dim(block, 0, width, axis=dim), axis, backward)
        block = jnp.concatenate([low, block, high], axis=dim)
    return block


def gelu_tanh(values):
    tanh_arg = slope_coef * (values + cubic_coef * values * values * values)
    return 0.5 * values * (1.0 + jnp.tanh(tanh_arg))


def gelu_slope(values):
    tangent = jnp.tanh(slope_coef * (values + cubic_coef * values * values * values))
    return 0.5 * (1.0 + tangent) + 0.5 * values * (1.0 - tangent * tangent) * slope_coef * (
        1.0 + 3.0 * cubic_coef * values * values
    )


def apply_stencil(padded, dw_weight, tile_rows, tile_cols, flipped):
    kernel_size = dw_weight.shape[0]
    result = jnp.zeros((padded.shape[0], tile_rows, tile_cols, padded.shape[3]), jnp.float32)
    for row_off in range(kernel_size):
        for col_off in range(kernel_size):
            row_start = kernel_size - 1 - row_off if flipped else row_off
            col_start = kernel_size - 1 - col_off if flipped else col_off
            result = (
                result
                + dw_weight[row_off, col_off]
                * padded[:, row_start : row_start + tile_rows, col_start : col_start + tile_cols]
            )
    return result


def local(student, teacher, dw_weight, norm_gain, w_in, w_out, layer_scale):
    batch_size, tile_rows, tile_cols, channel_count = student.shape
    kernel_size = dw_weight.shape[0]
    half_kernel = kernel_size // 2
    cell_total = batch_size * tile_rows * lax.axis_size("lat") * tile_cols * lax.axis_size("lon")
    lon_padded = with_halo(student, (("lon", 2),), half_kernel, True)
    padded_bf = with_halo(lon_padded, (("lat", 1),), half_kernel, False)
    padded = padded_bf.astype(jnp.float32)
    smoothed = apply_stencil(padded, dw_weight, tile_rows, tile_cols, False).reshape(
        -1, channel_count
    )
    average = jnp.mean(smoothed, axis=-1, keepdims=True)
    centred = smoothed - average
    variance = jnp.mean(centred * centred, axis=-1, keepdims=True)
    inv_std = lax.rsqrt(variance + norm_eps)
    unit_norm = centred * inv_std
    normed = (unit_norm * norm_gain).astype(jnp.bfloat16)
    preact = jnp.dot(normed, w_in, preferred_element_type=jnp.float32)
    hidden = gelu_tanh(preact).astype(jnp.bfloat16)
    mlp_out = jnp.dot(hidden, w_out, preferred_element_type=jnp.float32)
    output = student.reshape(-1, channel_count).astype(jnp.float32) + layer_scale * mlp_out
    target = lax.all_to_all(teacher, "lat", split_axis=1, concat_axis=2, tiled=True)
    misfit = output - target.reshape(-1, channel_count).astype(jnp.float32)
    out_grad = (layer_scale * misfit).astype(jnp.bfloat16)
    part_out = lax.dot_general(
        hidden, out_grad, (((0,), (0,)), ((), ())), preferred_element_type=jnp.float32
    )
    hidden_grad = lax.dot_general(
        out_grad, w_out, (((1,), (1,)), ((), ())), preferred_element_type=jnp.float32
    )
    preact_grad = (hidden_grad * gelu_slope(preact)).astype(jnp.bfloat16)
    part_in = lax.dot_general(
        normed, preact_grad, (((0,), (0,)), ((), ())), preferred_element_type=jnp.float32
    )
    normed_grad = lax.dot_general(
        preact_grad, w_in, (((1,), (1,)), ((), ())), preferred_element_type=jnp.float32
    )
    unit_grad = normed_grad * norm_gain
    first_mean = jnp.mean(unit_grad, axis=-1, keepdims=True)
    second_mean = jnp.mean(unit_grad * unit_norm, axis=-1, keepdims=True)
    conv_grad = (inv_std * (unit_grad - first_mean - unit_norm * second_mean)).astype(jnp.bfloat16)
    conv_grid = conv_grad.reshape(student.shape)
    grad_lon = with_halo(conv_grid, (("lon", 2),), half_kernel, True)
    padded_grad = with_halo(grad_lon, (("lat", 1),), half_kernel, False).astype(jnp.float32)
    back_conv = apply_stencil(padded_grad, dw_weight, tile_rows, tile_cols, True)
    grad_student = (misfit.reshape(student.shape) + back_conv).astype(jnp.bfloat16)
    conv_grad_f = conv_grid.astype(jnp.float32)
    kernel_terms = []
    for row_off in range(kernel_size):
        for col_off in range(kernel_size):
            kernel_terms.append(
                jnp.sum(
                    padded[:, row_off : row_off + tile_rows, col_off : col_off + tile_cols]
                    * conv_grad_f,
                    axis=(0, 1, 2),
                )
            )
    part_dw = jnp.stack(kernel_terms).reshape(kernel_size, kernel_size, channel_count)
    sum_in, sum_out, sum_dw = lax.psum((part_in, part_out, part_dw), ("lat", "lon"))
    return (grad_student, sum_in / cell_total, sum_out / cell_total, sum_dw / cell_total)


def solution(mesh):
    placed = (
        P(None, "lat", "lon", None),
        P(None, None, ("lon", "lat"), None),
        P(),
        P(),
        P(),
        P(),
        P(),
    )
    return jax.shard_map(
        local,
        mesh=mesh,
        in_specs=placed,
        out_specs=(P(None, "lat", "lon", None), P(), P(), P()),
        check_vma=False,
    )
```

profile of v0, /device:TPU:1, one launch (start us, length us, event | category | flops | bytes accessed | tf_op | source)
XLA Modules:
  0.0 569.1 jit_solution(4900694562744893407)
XLA Ops:
  7.2 0.9 fusion.114
  8.0 16.3 %collective-permute-start = (bf16[2,4,3,256]{3,2,1,0:T(4,128)(2,1)S(1)}, bf16[2,4,3,256]{3,2,1,0:T(4,128)(2,1)S(1)}, u32[]{:S(2)}, u32[]{:S(2)}) collective-permute-start(bf16[2,4,3,256]{3,2,1,0:T(4,128)(2,1)S(1)} %get-tuple-element.66), channel_id=1, source_target_pairs={{0,1},{1,2},{2,3},{3,4},{4,5},{5,6},{6,7},{7,8},{8,9},{9,10},{10,1... | collective-permute-start | bytes 36872 | tf_op jit(solution)/shard_map/ppermute | solution.py:18
  24.3 6.6 %collective-permute-start.1 = (bf16[2,4,3,256]{3,2,1,0:T(4,128)(2,1)S(1)}, bf16[2,4,3,256]{3,2,1,0:T(4,128)(2,1)S(1)}, u32[]{:S(2)}, u32[]{:S(2)}) collective-permute-start(bf16[2,4,3,256]{3,2,1,0:T(4,128)(2,1)S(1)} %get-tuple-element.67), channel_id=1, source_target_pairs={{1,0},{2,1},{3,2},{4,3},{5,4},{6,5},{7,6},{8,7},{9,8},{10,9},{11,1... | collective-permute-start | bytes 36872 | tf_op jit(solution)/shard_map/ppermute | solution.py:21
  30.9 1.7 copy.12
  32.5 10.1 %all-to-all-start = ((bf16[2,64,2,256]{3,2,0,1:T(2,128)(2,1)}), bf16[2,64,2,256]{3,2,0,1:T(2,128)(2,1)S(1)}, u32[]{:S(2)}, u32[]{:S(2)}) async-start(bf16[2,64,2,256]{3,2,0,1:T(2,128)(2,1)} %copy.12), calls=%async_computation | async-start | bytes 262144 | tf_op jit(solution)/shard_map/all_to_all | solution.py:74
  42.6 0.0 all-reduce.3.cloned.1.call-start
  42.9 0.1 pad_maximum_fusion
  43.0 3.5 collective-permute-start.2
  46.5 1.9 collective-permute-start.3
  48.6 4.7 collective-permute-done.3
  53.3 0.1 maximum_convert_fusion
  53.6 1.9 fusion.110
  55.5 0.1 div.33
  55.6 0.2 multiply_reduce_fusion.1
  55.8 0.1 rsqrt.12
  55.9 0.6 copy-done.50
  56.5 0.1 multiply_convert_fusion.3
  56.6 0.3 fusion.118
  57.0 0.1 copy_bitcast_fusion
  57.1 0.2 reshape.125
  57.3 0.7 copy-done.53
  57.9 1.6 fusion.2
  59.5 0.8 fusion
  60.3 0.5 fusion.109
  60.8 0.6 fusion.56
  61.5 0.5 fusion.38
  62.0 0.4 fusion.20
  62.4 1.6 fusion.108
  64.0 1.3 fusion.119
  65.3 0.2 stack.199
  65.5 3.7 collective-permute-start.4
  69.2 14.5 %collective-permute-start.5 = (bf16[2,4,3,256]{3,2,1,0:T(4,128)(2,1)S(1)}, bf16[2,4,3,256]{3,2,1,0:T(4,128)(2,1)S(1)}, u32[]{:S(2)}, u32[]{:S(2)}) collective-permute-start(bf16[2,4,3,256]{3,2,1,0:T(4,128)(2,1)S(1)} %get-tuple-element.65), channel_id=1, source_target_pairs={{1,0},{2,1},{3,2},{4,3},{5,4},{6,5},{7,6},{8,7},{9,8},{10,9},{11,1... | collective-permute-start | bytes 36872 | tf_op jit(solution)/shard_map/ppermute | solution.py:21
  83.7 101.0 %psum.23 = f32[7,7,256]{2,1,0:T(8,128)S(1)} all-reduce(f32[7,7,256]{2,1,0:T(8,128)S(1)} %reshape.123), channel_id=1, replica_groups=mesh['lat'=16,'lon'=32] {'lat','lon'}, use_global_device_ids=true, to_apply=%region_55.0 | all-reduce | flops 12544 | bytes 100352 | tf_op jit(solution)/shard_map/psum | solution.py:111
  184.7 0.1 pad_maximum_fusion.1
  184.8 2.5 collective-permute-start.6
  187.4 1.9 collective-permute-start.7
  189.3 0.6 broadcast_multiply_fusion.2
  189.9 3.6 collective-permute-done.7
  193.8 0.1 maximum_convert_fusion.1
  193.8 0.3 copy-done.7
  194.2 0.1 copy-done.9
  194.2 0.0 copy-done.17
  194.4 0.0 copy-done.49
  194.4 0.1 copy-done.5
  194.5 2.4 fusion.59
  196.9 361.8 %all-reduce.3.cloned.1.call-done = (f32[256,1024]{1,0:T(8,128)}, f32[1024,256]{1,0:T(8,128)}) async-done(((f32[256,1024]{1,0:T(8,128)}, f32[1024,256]{1,0:T(8,128)}), (f32[256,1024]{1,0:T(8,128)}, f32[1024,256]{1,0:T(8,128)})) %all-reduce.3.cloned.1.call-update) | async-done | bytes 2097168 | tf_op jit(solution)/shard_map/psum | solution.py:111
  558.8 2.4 broadcast_multiply_fusion
  561.1 1.1 broadcast_multiply_fusion.1
  (119 shorter events, 0.5 us)
Async XLA Ops:
  7.2 49.5 %copy-start = (bf16[256,1024]{1,0:T(8,128)(2,1)S(1)}, bf16[256,1024]{1,0:T(8,128)(2,1)}, u32[]{:S(2)}) copy-start(bf16[256,1024]{1,0:T(8,128)(2,1)} %param.11) | copy-start | bytes 1572868
  8.0 34.8 %collective-permute-start = (bf16[2,4,3,256]{3,2,1,0:T(4,128)(2,1)S(1)}, bf16[2,4,3,256]{3,2,1,0:T(4,128)(2,1)S(1)}, u32[]{:S(2)}, u32[]{:S(2)}) collective-permute-start(bf16[2,4,3,256]{3,2,1,0:T(4,128)(2,1)S(1)} %get-tuple-element.66), channel_id=1, source_target_pairs={{0,1},{1,2},{2,3},{3,4},{4,5},{5,6},{6,7},{7,8},{8,9},{9,10},{10,1... | collective-permute-start | bytes 36872 | tf_op jit(solution)/shard_map/ppermute | solution.py:18
  24.3 18.6 %collective-permute-start.1 = (bf16[2,4,3,256]{3,2,1,0:T(4,128)(2,1)S(1)}, bf16[2,4,3,256]{3,2,1,0:T(4,128)(2,1)S(1)}, u32[]{:S(2)}, u32[]{:S(2)}) collective-permute-start(bf16[2,4,3,256]{3,2,1,0:T(4,128)(2,1)S(1)} %get-tuple-element.67), channel_id=1, source_target_pairs={{1,0},{2,1},{3,2},{4,3},{5,4},{6,5},{7,6},{8,7},{9,8},{10,9},{11,1... | collective-permute-start | bytes 36872 | tf_op jit(solution)/shard_map/ppermute | solution.py:21
  32.5 10.2 %copy-start.3 = (f32[7,7,256]{2,1,0:T(8,128)S(1)}, f32[7,7,256]{2,1,0:T(8,128)}, u32[]{:S(2)}) copy-start(f32[7,7,256]{2,1,0:T(8,128)} %param.9) | copy-start | bytes 150532
  32.5 10.4 %copy-start.2 = (bf16[2,4,32,256]{3,2,1,0:T(8,128)(2,1)S(1)}, bf16[2,4,32,256]{3,2,1,0:T(8,128)(2,1)}, u32[]{:S(2)}) copy-start(bf16[2,4,32,256]{3,2,1,0:T(8,128)(2,1)} %param.7) | copy-start | bytes 393220
  32.5 24.4 %all-to-all-start = ((bf16[2,64,2,256]{3,2,0,1:T(2,128)(2,1)}), bf16[2,64,2,256]{3,2,0,1:T(2,128)(2,1)S(1)}, u32[]{:S(2)}, u32[]{:S(2)}) async-start(bf16[2,64,2,256]{3,2,0,1:T(2,128)(2,1)} %copy.12), calls=%async_computation | async-start | bytes 262144 | tf_op jit(solution)/shard_map/all_to_all | solution.py:74
  42.6 516.1 %all-reduce.3.cloned.1.call-start = ((), (), s32[]{:S(2)}) async-start(), calls=%async_computation.1 | async-start | bytes 4194304 | tf_op jit(solution)/shard_map/psum | solution.py:111
  42.8 10.7 %copy-start.4 = (f32[1,1,256]{2,1,0:T(1,128)}, f32[1,1,256]{2,1,0:T(1,128)S(1)}, u32[]{:S(2)}) copy-start(f32[1,1,256]{2,1,0:T(1,128)S(1)} %get-tuple-element.94) | copy-start | bytes 3076
  42.8 10.7 %copy-start.6 = (f32[1,1,256]{2,1,0:T(1,128)}, f32[1,1,256]{2,1,0:T(1,128)S(1)}, u32[]{:S(2)}) copy-start(f32[1,1,256]{2,1,0:T(1,128)S(1)} %get-tuple-element.95) | copy-start | bytes 3076
  42.8 10.7 %copy-start.8 = (f32[1,1,256]{2,1,0:T(1,128)}, f32[1,1,256]{2,1,0:T(1,128)S(1)}, u32[]{:S(2)}) copy-start(f32[1,1,256]{2,1,0:T(1,128)S(1)} %get-tuple-element.96) | copy-start | bytes 3076
  42.8 10.7 %copy-start.10 = (f32[1,1,256]{2,1,0:T(1,128)}, f32[1,1,256]{2,1,0:T(1,128)S(1)}, u32[]{:S(2)}) copy-start(f32[1,1,256]{2,1,0:T(1,128)S(1)} %get-tuple-element.97) | copy-start | bytes 3076
  42.8 10.7 %copy-start.12 = (f32[1,1,256]{2,1,0:T(1,128)}, f32[1,1,256]{2,1,0:T(1,128)S(1)}, u32[]{:S(2)}) copy-start(f32[1,1,256]{2,1,0:T(1,128)S(1)} %get-tuple-element.98) | copy-start | bytes 3076
  42.8 10.7 %copy-start.14 = (f32[1,1,256]{2,1,0:T(1,128)}, f32[1,1,256]{2,1,0:T(1,128)S(1)}, u32[]{:S(2)}) copy-start(f32[1,1,256]{2,1,0:T(1,128)S(1)} %get-tuple-element.99) | copy-start | bytes 3076
  42.8 10.7 %copy-start.16 = (f32[1,1,256]{2,1,0:T(1,128)}, f32[1,1,256]{2,1,0:T(1,128)S(1)}, u32[]{:S(2)}) copy-start(f32[1,1,256]{2,1,0:T(1,128)S(1)} %get-tuple-element.100) | copy-start | bytes 3076
  42.8 10.7 %copy-start.18 = (f32[1,1,256]{2,1,0:T(1,128)}, f32[1,1,256]{2,1,0:T(1,128)S(1)}, u32[]{:S(2)}) copy-start(f32[1,1,256]{2,1,0:T(1,128)S(1)} %get-tuple-element.101) | copy-start | bytes 3076
  42.8 10.7 %copy-start.20 = (f32[1,1,256]{2,1,0:T(1,128)}, f32[1,1,256]{2,1,0:T(1,128)S(1)}, u32[]{:S(2)}) copy-start(f32[1,1,256]{2,1,0:T(1,128)S(1)} %get-tuple-element.102) | copy-start | bytes 3076
  42.8 10.7 %copy-start.22 = (f32[1,1,256]{2,1,0:T(1,128)}, f32[1,1,256]{2,1,0:T(1,128)S(1)}, u32[]{:S(2)}) copy-start(f32[1,1,256]{2,1,0:T(1,128)S(1)} %get-tuple-element.103) | copy-start | bytes 3076
  42.9 10.7 %copy-start.24 = (f32[1,1,256]{2,1,0:T(1,128)}, f32[1,1,256]{2,1,0:T(1,128)S(1)}, u32[]{:S(2)}) copy-start(f32[1,1,256]{2,1,0:T(1,128)S(1)} %get-tuple-element.104) | copy-start | bytes 3076
  42.9 10.7 %copy-start.26 = (f32[1,1,256]{2,1,0:T(1,128)}, f32[1,1,256]{2,1,0:T(1,128)S(1)}, u32[]{:S(2)}) copy-start(f32[1,1,256]{2,1,0:T(1,128)S(1)} %get-tuple-element.105) | copy-start | bytes 3076
  43.0 5.6 collective-permute-start.2
  46.5 6.8 %collective-permute-start.3 = (bf16[2,3,38,256]{3,2,1,0:T(8,128)(2,1)S(1)}, bf16[2,3,38,256]{3,2,1,0:T(8,128)(2,1)S(1)}, u32[]{:S(2)}, u32[]{:S(2)}) collective-permute-start(bf16[2,3,38,256]{3,2,1,0:T(8,128)(2,1)S(1)} %get-tuple-element.63), channel_id=1, source_target_pairs={{32,0},{64,32},{96,64},{128,96},{160,128},{192,160},{224,192},{256... | collective-permute-start | bytes 350216 | tf_op jit(solution)/shard_map/ppermute | solution.py:21
  48.5 5.0 copy-start.28
  48.5 5.0 copy-start.30
  48.5 5.0 copy-start.32
  48.5 5.0 copy-start.34
  48.5 5.0 copy-start.36
  48.5 5.0 copy-start.38
  48.6 5.0 copy-start.40
  48.6 5.0 copy-start.42
  48.6 5.0 copy-start.44
  48.6 5.0 copy-start.46
  48.6 5.0 copy-start.48
  55.8 0.7 copy-start.50
  57.2 0.7 copy-start.53
  57.9 1.6 copy-start.52
  59.5 0.8 copy-start.51
  65.5 119.3 %collective-permute-start.4 = (bf16[2,4,3,256]{3,2,1,0:T(4,128)(2,1)S(1)}, bf16[2,4,3,256]{3,2,1,0:T(4,128)(2,1)S(1)}, u32[]{:S(2)}, u32[]{:S(2)}) collective-permute-start(bf16[2,4,3,256]{3,2,1,0:T(4,128)(2,1)S(1)} %get-tuple-element.64), channel_id=1, source_target_pairs={{0,1},{1,2},{2,3},{3,4},{4,5},{5,6},{6,7},{7,8},{8,9},{9,10},{10,1... | collective-permute-start | bytes 36872 | tf_op jit(solution)/shard_map/ppermute | solution.py:18
  69.2 115.5 %collective-permute-start.5 = (bf16[2,4,3,256]{3,2,1,0:T(4,128)(2,1)S(1)}, bf16[2,4,3,256]{3,2,1,0:T(4,128)(2,1)S(1)}, u32[]{:S(2)}, u32[]{:S(2)}) collective-permute-start(bf16[2,4,3,256]{3,2,1,0:T(4,128)(2,1)S(1)} %get-tuple-element.65), channel_id=1, source_target_pairs={{1,0},{2,1},{3,2},{4,3},{5,4},{6,5},{7,6},{8,7},{9,8},{10,9},{11,1... | collective-permute-start | bytes 36872 | tf_op jit(solution)/shard_map/ppermute | solution.py:21
  184.8 5.1 collective-permute-start.6
  187.4 6.2 %collective-permute-start.7 = (bf16[2,3,38,256]{3,2,1,0:T(8,128)(2,1)S(1)}, bf16[2,3,38,256]{3,2,1,0:T(8,128)(2,1)S(1)}, u32[]{:S(2)}, u32[]{:S(2)}) collective-permute-start(bf16[2,3,38,256]{3,2,1,0:T(8,128)(2,1)S(1)} %get-tuple-element.61), channel_id=1, source_target_pairs={{32,0},{64,32},{96,64},{128,96},{160,128},{192,160},{224,192},{256... | collective-permute-start | bytes 350216 | tf_op jit(solution)/shard_map/ppermute | solution.py:21
  193.6 0.7 copy-start.13
  193.6 0.7 copy-start.17
  193.6 0.7 copy-start.19
  193.6 0.7 copy-start.27
  193.7 0.7 copy-start.39
  193.7 0.7 copy-start.49
  193.8 0.7 copy-start.5
  558.8 2.4 copy-start.1
  (16 other events, 10.6 us)
Sparse Core Ops, SparseCore 0:
  83.8 474.8 all-reduce.2
where the time goes:
time: 570 us; the launch traced here: 569 us
  waiting for transfers between devices  370 us (65%)
  blocking collectives  101 us (18%)
  starting transfers between devices  61.1 us (11%)
  between operations  14.9 us (3%)
  other arithmetic  10.6 us (2%)
  matrix products  5.99 us (1%)
    psum x1, waiting for transfers between devices, local(): lax.psum((part_in, part_out, part_dw), ('lat', 'lon'))  362 us
    psum x1, blocking collectives, local(): lax.psum((part_in, part_out, part_dw), ('lat', 'lon'))  101 us
    ppermute x4, starting transfers between devices, with_halo(): lax.ppermute(lax.slice_in_dim(block, block.shape[dim] - width, None, axis...  26.1 us
    ppermute x4, starting transfers between devices, with_halo(): lax.ppermute(lax.slice_in_dim(block, 0, width, axis=dim), axis, backward)  24.9 us
  transfers between devices with their start and end apart: 10, of which 3 were waited for; matrix products, arithmetic and copies ran while one was open for 1% of the time, Pallas kernels for 0%

commit v1 on v0

--- a/solution.py
+++ b/solution.py
@@ -1,11 +1,225 @@
 import jax
 import jax.numpy as jnp
 from jax import lax
+from jax.experimental import pallas as pl
+from jax.experimental.pallas import tpu as pltpu
 from jax.sharding import PartitionSpec as P
 
 slope_coef = 0.7978845608028654
 cubic_coef = 0.044715
 norm_eps = 1e-06
+MESH = pl.DeviceIdType.MESH
+
+BLOCKS, SIDE, SPLIT, TILE, DW_ROWS, DW_PAD = 16, 128, 64, 8, 4, 16
+LOWER = SIDE - SPLIT + DW_PAD
+CHIPS_Z = 16
+
+
+def sum_kernel(
+    left_a, right_a, left_b, right_b, dw_ref, out_a, out_b, out_dw,
+    own, other, dw_other, top, low, top_in1, low_in1, top1, low1, top_in2, low_in2,
+    z_send, z_in, z_own, z_all, top_g1, low_g1, top_all, low_all,
+    core_ssem, core_rsem, xy_ssem, xy_rsem, z_ssem, z_rsem,
+):
+    lat, lon = lax.axis_index("lat"), lax.axis_index("lon")
+    core = lax.rem(lat, 2)
+    z = lax.rem(lon, 2) * 8 + lat // 2
+    x = lon // 8
+    y = lax.rem(lon // 2, 4)
+
+    def device(core_to, z_to, x_to, y_to):
+        return {
+            "lat": lax.rem(z_to, 8) * 2 + core_to,
+            "lon": x_to * 8 + y_to * 2 + z_to // 8,
+        }
+
+    partner = device(1 - core, z, x, y)
+    x_peers = [lax.rem(x + d, 4) for d in range(4)]
+    y_peers = [lax.rem(y + d, 4) for d in range(4)]
+    z_peers = [lax.rem(z + d, CHIPS_Z) for d in range(CHIPS_Z)]
+    x_devices = [device(core, z, p, y) for p in x_peers]
+    y_devices = [device(core, z, x, p) for p in y_peers]
+    z_devices = [device(core, p, x, y) for p in z_peers]
+
+    barrier = pltpu.get_barrier_semaphore()
+    friends = [partner] + x_devices[1:] + y_devices[1:] + z_devices[1:]
+    for friend in friends:
+        pl.semaphore_signal(barrier, inc=1, device_id=friend, device_id_type=MESH)
+
+    def send(source, target, ssem, rsem, device_to):
+        copy = pltpu.make_async_remote_copy(
+            src_ref=source, dst_ref=target, send_sem=ssem, recv_sem=rsem,
+            device_id=device_to, device_id_type=MESH,
+        )
+        copy.start()
+        return copy
+
+    for which, (left, right) in enumerate(((left_a, right_a), (left_b, right_b))):
+        product = lax.dot_general(
+            left[...], right[...], (((0,), (0,)), ((), ())), preferred_element_type=jnp.float32
+        )
+        for block in range(BLOCKS):
+            row, col = SIDE * (block // 8), SIDE * (block % 8)
+            own[which, block] = product[row : row + SIDE, col : col + SIDE]
+    pl.semaphore_wait(barrier, len(friends))
+
+    copies = [
+        send(own.at[1 - core], other, core_ssem.at[0], core_rsem.at[0], partner),
+        send(dw_ref.at[1 - core], dw_other, core_ssem.at[1], core_rsem.at[1], partner),
+    ]
+    for copy in copies:
+        copy.wait()
+    for block in range(BLOCKS):
+        bx, by = block // 4, block % 4
+        top[bx, by] = own[core, block, :SPLIT] + other[block, :SPLIT]
+        low[by, bx, : SIDE - SPLIT] = own[core, block, SPLIT:] + other[block, SPLIT:]
+        rows = slice(DW_ROWS * block, DW_ROWS * (block + 1))
+        dw_sum = dw_ref[core, rows] + dw_other[rows]
+        low[by, bx, SIDE - SPLIT :] = jnp.concatenate(
+            [dw_sum, jnp.zeros((DW_PAD - DW_ROWS, SIDE), jnp.float32)], axis=0
+        )
+
+    copies = []
+    for d in (2, 1, 3):
+        copies.append(
+            send(top.at[x_peers[d]], top_in1.at[d], xy_ssem.at[0, d], xy_rsem.at[0, d], x_devices[d])
+        )
+        copies.append(
+            send(low.at[y_peers[d]], low_in1.at[d], xy_ssem.at[1, d], xy_rsem.at[1, d], y_devices[d])
+        )
+    for copy in copies:
+        copy.wait()
+    top1[...] = top[x] + top_in1[1] + top_in1[2] + top_in1[3]
+    low1[...] = low[y] + low_in1[1] + low_in1[2] + low_in1[3]
+
+    copies = []
+    for d in (2, 1, 3):
+        copies.append(
+            send(top1.at[y_peers[d]], top_in2.at[d], xy_ssem.at[2, d], xy_rsem.at[2, d], y_devices[d])
+        )
+        copies.append(
+            send(low1.at[x_peers[d]], low_in2.at[d], xy_ssem.at[3, d], xy_rsem.at[3, d], x_devices[d])
+        )
+    for copy in copies:
+        copy.wait()
+    top2 = top1[y] + top_in2[1] + top_in2[2] + top_in2[3]
+    low2 = low1[x] + low_in2[1] + low_in2[2] + low_in2[3]
+    for tile in range(CHIPS_Z):
+        at = TILE * tile
+        z_send[tile, :TILE] = top2[at : at + TILE] if at < SPLIT else low2[at - SPLIT : at - SPLIT + TILE]
+        z_send[tile, TILE:] = low2[SIDE - SPLIT : SIDE - SPLIT + TILE]
+
+    order = [8, 7, 9, 6, 10, 5, 11, 4, 12, 3, 13, 2, 14, 1, 15]
+    copies = []
+    for d in order:
+        copies.append(
+            send(z_send.at[z_peers[d]], z_in.at[z], z_ssem.at[0, d], z_rsem.at[0, d], z_devices[d])
+        )
+    z_in[z] = z_send[z]
+    for copy in copies:
+        copy.wait()
+    total = z_in[0]
+    for tile in range(1, CHIPS_Z):
+        total = total + z_in[tile]
+    z_own[...] = total
+
+    copies = []
+    for d in order:
+        copies.append(
+            send(z_own.at[:TILE], z_all.at[z], z_ssem.at[1, d], z_rsem.at[1, d], z_devices[d])
+        )
+    z_all[z] = z_own[:TILE]
+    for copy in copies:
+        copy.wait()
+    tiles = z_all[...].reshape(SIDE, SIDE)
+    dw_tile = jnp.concatenate(
+        [z_own[TILE:], jnp.zeros((DW_PAD - TILE, SIDE), jnp.float32)], axis=0
+    )
+    top_g1[y] = tiles[:SPLIT].astype(jnp.bfloat16)
+    low_g1[x] = jnp.concatenate([tiles[SPLIT:], dw_tile], axis=0).astype(jnp.bfloat16)
+
+    copies = []
+    for d in (2, 1, 3):
+        copies.append(
+            send(top_g1.at[y], top_g1.at[y], xy_ssem.at[4, d], xy_rsem.at[4, d], y_devices[d])
+        )
+        copies.append(
+            send(low_g1.at[x], low_g1.at[x], xy_ssem.at[5, d], xy_rsem.at[5, d], x_devices[d])
+        )
+    for copy in copies:
+        copy.wait()
+
+    copies = []
+    for d in (2, 1, 3):
+        copies.append(
+            send(top_g1, top_all.at[core, x], xy_ssem.at[6, d], xy_rsem.at[6, d], x_devices[d])
+        )
+        copies.append(
+            send(low_g1, low_all.at[core, y], xy_ssem.at[7, d], xy_rsem.at[7, d], y_devices[d])
+        )
+    top_all[core, x] = top_g1[...]
+    low_all[core, y] = low_g1[...]
+    for copy in copies:
+        copy.wait()
+
+    copies = [
+        send(top_all.at[core], top_all.at[core], core_ssem.at[2], core_rsem.at[2], partner),
+        send(low_all.at[core], low_all.at[core], core_ssem.at[3], core_rsem.at[3], partner),
+    ]
+    for copy in copies:
+        copy.wait()
+    for which, out in enumerate((out_a, out_b)):
+        for block in range(BLOCKS):
+            bx, by = block // 4, block % 4
+            row, col = SIDE * (block // 8), SIDE * (block % 8)
+            out[row : row + SPLIT, col : col + SIDE] = top_all[which, bx, by]
+            out[row + SPLIT : row + SIDE, col : col + SIDE] = low_all[which, by, bx, : SIDE - SPLIT]
+            dw_rows = low_all[which, by, bx, SIDE - SPLIT :].astype(jnp.float32)[:DW_ROWS]
+            out_dw[which, DW_ROWS * block : DW_ROWS * (block + 1)] = dw_rows
+
+
+def sum_gradients(left_a, right_a, left_b, right_b, dw):
+    f32, bf16 = jnp.float32, jnp.bfloat16
+    vmem = pl.BlockSpec(memory_space=pltpu.VMEM)
+    shape = (left_a.shape[1], right_a.shape[1])
+    return pl.pallas_call(
+        sum_kernel,
+        out_shape=(
+            jax.ShapeDtypeStruct(shape, bf16),
+            jax.ShapeDtypeStruct(shape, bf16),
+            jax.ShapeDtypeStruct(dw.shape, f32),
+        ),
+        in_specs=[vmem] * 5,
+        out_specs=(vmem,) * 3,
+        scratch_shapes=[
+            pltpu.VMEM((2, BLOCKS, SIDE, SIDE), f32),
+            pltpu.VMEM((BLOCKS, SIDE, SIDE), f32),
+            pltpu.VMEM(dw.shape[1:], f32),
+            pltpu.VMEM((4, 4, SPLIT, SIDE), f32),
+            pltpu.VMEM((4, 4, LOWER, SIDE), f32),
+            pltpu.VMEM((4, 4, SPLIT, SIDE), f32),
+            pltpu.VMEM((4, 4, LOWER, SIDE), f32),
+            pltpu.VMEM((4, SPLIT, SIDE), f32),
+            pltpu.VMEM((4, LOWER, SIDE), f32),
+            pltpu.VMEM((4, SPLIT, SIDE), f32),
+            pltpu.VMEM((4, LOWER, SIDE), f32),
+            pltpu.VMEM((CHIPS_Z, 2 * TILE, SIDE), f32),
+            pltpu.VMEM((CHIPS_Z, 2 * TILE, SIDE), f32),
+            pltpu.VMEM((2 * TILE, SIDE), f32),
+            pltpu.VMEM((CHIPS_Z, TILE, SIDE), f32),
+            pltpu.VMEM((4, SPLIT, SIDE), bf16),
+            pltpu.VMEM((4, LOWER, SIDE), bf16),
+            pltpu.VMEM((2, 4, 4, SPLIT, SIDE), bf16),
+            pltpu.VMEM((2, 4, 4, LOWER, SIDE), bf16),
+            pltpu.SemaphoreType.DMA((4,)),
+            pltpu.SemaphoreType.DMA((4,)),
+            pltpu.SemaphoreType.DMA((8, 4)),
+            pltpu.SemaphoreType.DMA((8, 4)),
+            pltpu.SemaphoreType.DMA((2, CHIPS_Z)),
+            pltpu.SemaphoreType.DMA((2, CHIPS_Z)),
+        ],
+        compiler_params=pltpu.CompilerParams(collective_id=0, has_side_effects=True),
+    )(left_a, right_a, left_b, right_b, dw)
 
 
 def with_halo(block, sides, width, periodic):
@@ -74,16 +288,10 @@
     target = lax.all_to_all(teacher, "lat", split_axis=1, concat_axis=2, tiled=True)
     misfit = output - target.reshape(-1, channel_count).astype(jnp.float32)
     out_grad = (layer_scale * misfit).astype(jnp.bfloat16)
-    part_out = lax.dot_general(
-        hidden, out_grad, (((0,), (0,)), ((), ())), preferred_element_type=jnp.float32
-    )
     hidden_grad = lax.dot_general(
         out_grad, w_out, (((1,), (1,)), ((), ())), preferred_element_type=jnp.float32
     )
     preact_grad = (hidden_grad * gelu_slope(preact)).astype(jnp.bfloat16)
-    part_in = lax.dot_general(
-        normed, preact_grad, (((0,), (0,)), ((), ())), preferred_element_type=jnp.float32
-    )
     normed_grad = lax.dot_general(
         preact_grad, w_in, (((1,), (1,)), ((), ())), preferred_element_type=jnp.float32
     )
@@ -107,9 +315,17 @@
                     axis=(0, 1, 2),
                 )
             )
-    part_dw = jnp.stack(kernel_terms).reshape(kernel_size, kernel_size, channel_count)
-    sum_in, sum_out, sum_dw = lax.psum((part_in, part_out, part_dw), ("lat", "lon"))
-    return (grad_student, sum_in / cell_total, sum_out / cell_total, sum_dw / cell_total)
+    taps = kernel_size * kernel_size
+    part_dw = jnp.pad(jnp.stack(kernel_terms), ((0, BLOCKS * DW_ROWS - taps), (0, 0)))
+    part_dw = part_dw.reshape(BLOCKS * DW_ROWS, 2, SIDE).transpose(1, 0, 2)
+    sum_in, sum_out, sum_dw = sum_gradients(normed, preact_grad, out_grad, hidden, part_dw)
+    sum_dw = sum_dw.transpose(1, 0, 2)[:taps].reshape(kernel_size, kernel_size, channel_count)
+    return (
+        grad_student,
+        sum_in.astype(jnp.float32) / cell_total,
+        sum_out.T.astype(jnp.float32) / cell_total,
+        sum_dw / cell_total,
+    )
 
 
 def solution(mesh):

time: 570 us -> 151 us (0.26)
  waiting for transfers between devices: 370 us -> 18.6 us
  blocking collectives: 101 us -> 0 us
  Pallas kernels: 0 us -> 56.2 us
  between operations: 14.9 us -> 1.61 us
  starting transfers between devices: 61.1 us -> 54.6 us
    psum x1 -> x0, waiting for transfers between devices: 362 us -> none  [local(): lax.psum((part_in, part_out, part_dw), ('lat', 'lon'))]
    psum x1 -> x0, blocking collectives: 101 us -> none  [local(): lax.psum((part_in, part_out, part_dw), ('lat', 'lon'))]
    pallas_call x0 -> x1, Pallas kernels: none -> 56.2 us  [sum_gradients(): pl.pallas_call(sum_kernel, out_shape=(jax.ShapeDtypeStruct(shape, bf16),...]
    ppermute x4, waiting for transfers between devices: 0.01 us -> 18.1 us  [with_halo(): lax.ppermute(lax.slice_in_dim(block, block.shape[dim] - width, None, axis...]
    ppermute x4, waiting for transfers between devices: 8.37 us -> 0.5 us  [with_halo(): lax.ppermute(lax.slice_in_dim(block, 0, width, axis=dim), axis, backward)]
  transfers between devices with their start and end apart: 10 -> 9, of which waited for: 3 -> 4; matrix products, arithmetic and copies ran while one was open for 1% -> 6% of each run, Pallas kernels for 0% -> 37%
where the time goes in v1:
time: 151 us; the launch traced here: 150 us
  Pallas kernels  56.2 us (37%)
  starting transfers between devices  54.6 us (36%)
  waiting for transfers between devices  18.6 us (12%)
  other arithmetic  8.87 us (6%)
  local copies, waits for them, and re-layouts  7.61 us (5%)
  matrix products  2.93 us (2%)
  between operations  1.61 us (1%)
    pallas_call x1, Pallas kernels, sum_gradients(): pl.pallas_call(sum_kernel, out_shape=(jax.ShapeDtypeStruct(shape, bf16),...  56.2 us
    ppermute x4, starting transfers between devices, with_halo(): lax.ppermute(lax.slice_in_dim(block, block.shape[dim] - width, None, axis...  20.9 us
    ppermute x4, starting transfers between devices, with_halo(): lax.ppermute(lax.slice_in_dim(block, 0, width, axis=dim), axis, backward)  19.5 us
    ppermute x4, waiting for transfers between devices, with_halo(): lax.ppermute(lax.slice_in_dim(block, block.shape[dim] - width, None, axis...  18.1 us
    all_to_all x1, starting transfers between devices, local(): lax.all_to_all(teacher, 'lat', split_axis=1, concat_axis=2, tiled=True)  14.2 us
    unnamed x122, local copies, waits for them, and re-layouts  5.65 us
  transfers between devices with their start and end apart: 9, of which 4 were waited for; matrix products, arithmetic and copies ran while one was open for 6% of the time, Pallas kernels for 37%

profile of v1, /device:TPU:1, one launch (start us, length us, event | category | flops | bytes accessed | tf_op | source)
XLA Modules:
  0.0 150.4 jit_solution(2503477313416773864)
XLA Ops:
  0.6 1.7 %copy.17 = bf16[2,64,2,256]{3,2,0,1:T(2,128)(2,1)} copy(bf16[2,64,2,256]{3,2,1,0:T(2,128)(2,1)} %param.8) | data formatting | bytes 262144 | tf_op args[1]
  2.4 14.2 %all-to-all-start = ((bf16[2,64,2,256]{3,2,0,1:T(2,128)(2,1)}), bf16[2,64,2,256]{3,2,0,1:T(2,128)(2,1)S(1)}, u32[]{:S(2)}, u32[]{:S(2)}) async-start(bf16[2,64,2,256]{3,2,0,1:T(2,128)(2,1)} %copy.17), calls=%async_computation | async-start | bytes 262144 | tf_op jit(solution)/shard_map/all_to_all | solution.py:288
  16.6 12.6 %collective-permute-start.1 = (bf16[2,4,3,256]{3,2,1,0:T(4,128)(2,1)S(1)}, bf16[2,4,3,256]{3,2,1,0:T(4,128)(2,1)S(1)}, u32[]{:S(2)}, u32[]{:S(2)}) collective-permute-start(bf16[2,4,3,256]{3,2,1,0:T(4,128)(2,1)S(1)} %get-tuple-element.83), channel_id=1, source_target_pairs={{1,0},{2,1},{3,2},{4,3},{5,4},{6,5},{7,6},{8,7},{9,8},{10,9},{11,1... | collective-permute-start | bytes 36872 | tf_op jit(solution)/shard_map/ppermute | solution.py:235
  29.2 1.9 %collective-permute-start = (bf16[2,4,3,256]{3,2,1,0:T(4,128)(2,1)S(1)}, bf16[2,4,3,256]{3,2,1,0:T(4,128)(2,1)S(1)}, u32[]{:S(2)}, u32[]{:S(2)}) collective-permute-start(bf16[2,4,3,256]{3,2,1,0:T(4,128)(2,1)S(1)} %get-tuple-element.82), channel_id=1, source_target_pairs={{0,1},{1,2},{2,3},{3,4},{4,5},{5,6},{6,7},{7,8},{8,9},{9,10},{10,1... | collective-permute-start | bytes 36872 | tf_op jit(solution)/shard_map/ppermute | solution.py:232
  31.3 15.8 %collective-permute-done = bf16[2,4,3,256]{3,2,1,0:T(4,128)(2,1)S(1)} collective-permute-done((bf16[2,4,3,256]{3,2,1,0:T(4,128)(2,1)S(1)}, bf16[2,4,3,256]{3,2,1,0:T(4,128)(2,1)S(1)}, u32[]{:S(2)}, u32[]{:S(2)}) %collective-permute-start) | collective-permute-done | bytes 12320 | tf_op jit(solution)/shard_map/ppermute | solution.py:232
  47.1 0.1 pad_maximum_fusion
  47.1 3.0 %collective-permute-start.3 = (bf16[2,3,38,256]{3,2,1,0:T(8,128)(2,1)S(1)}, bf16[2,3,38,256]{3,2,1,0:T(8,128)(2,1)S(1)}, u32[]{:S(2)}, u32[]{:S(2)}) collective-permute-start(bf16[2,3,38,256]{3,2,1,0:T(8,128)(2,1)S(1)} %get-tuple-element.79), channel_id=1, source_target_pairs={{32,0},{64,32},{96,64},{128,96},{160,128},{192,160},{224,192},{256... | collective-permute-start | bytes 350216 | tf_op jit(solution)/shard_map/ppermute | solution.py:235
  50.1 3.4 %collective-permute-start.2 = (bf16[2,3,38,256]{3,2,1,0:T(8,128)(2,1)S(1)}, bf16[2,3,38,256]{3,2,1,0:T(8,128)(2,1)S(1)}, u32[]{:S(2)}, u32[]{:S(2)}) collective-permute-start(bf16[2,3,38,256]{3,2,1,0:T(8,128)(2,1)S(1)} %get-tuple-element.78), channel_id=1, source_target_pairs={{0,32},{32,64},{64,96},{96,128},{128,160},{160,192},{192,224},{224... | collective-permute-start | bytes 350216 | tf_op jit(solution)/shard_map/ppermute | solution.py:232
  53.7 0.5 collective-permute-done.3
  54.2 1.2 collective-permute-done.2
  55.4 0.1 maximum_convert_fusion
  55.7 1.8 %fusion.109 = (f32[2,4,32]{2,1,0:T(4,128)S(1)}, f32[2,4,32,256]{3,2,1,0:T(8,128)S(1)}) fusion(f32[2,10,38,256]{3,2,1,0:T(8,128)S(1)} %maximum_convert_fusion, f32[256]{0:T(256)S(1)} %bitcast.285, f32[256]{0:T(256)S(1)} %bitcast.287, f32[256]{0:T(256)S(1)} %bitcast.193, f32[256]{0:T(256)S(1)} %bitcast.195, f32[256]{0:T(256)S(1)} %bitcast.197, ...), kind=kLoop, calls=%fused_computation.234 | loop fusion | flops 6422272 | bytes 13158400 | tf_op jit(solution)/shard_map/reduce_sum | solution.py:278
  57.6 0.1 div.35
  57.7 0.2 multiply_reduce_fusion.1
  57.9 0.1 rsqrt.12
  58.0 0.6 copy-done.56
  58.6 0.1 multiply_convert_fusion.3.left_a
  58.7 1.4 multiply_convert_fusion
  60.1 0.1 copy_bitcast_fusion
  60.2 0.2 reshape.128
  60.4 0.9 copy-done.4
  61.3 0.3 multiply_convert_fusion.2
  61.7 0.1 copy-done.59
  61.7 0.8 fusion.right_a
  62.6 0.5 fusion.108
  63.0 0.3 copy-done.2
  63.3 0.6 fusion.56
  64.0 0.4 fusion.20
  64.4 0.5 fusion.38
  65.0 1.9 %collective-permute-start.5 = (bf16[2,4,3,256]{3,2,1,0:T(4,128)(2,1)S(1)}, bf16[2,4,3,256]{3,2,1,0:T(4,128)(2,1)S(1)}, u32[]{:S(2)}, u32[]{:S(2)}) collective-permute-start(bf16[2,4,3,256]{3,2,1,0:T(4,128)(2,1)S(1)} %get-tuple-element.81), channel_id=1, source_target_pairs={{1,0},{2,1},{3,2},{4,3},{5,4},{6,5},{7,6},{8,7},{9,8},{10,9},{11,1... | collective-permute-start | bytes 36872 | tf_op jit(solution)/shard_map/ppermute | solution.py:235
  66.9 12.1 %collective-permute-start.4 = (bf16[2,4,3,256]{3,2,1,0:T(4,128)(2,1)S(1)}, bf16[2,4,3,256]{3,2,1,0:T(4,128)(2,1)S(1)}, u32[]{:S(2)}, u32[]{:S(2)}) collective-permute-start(bf16[2,4,3,256]{3,2,1,0:T(4,128)(2,1)S(1)} %get-tuple-element.80), channel_id=1, source_target_pairs={{0,1},{1,2},{2,3},{3,4},{4,5},{5,6},{6,7},{7,8},{8,9},{9,10},{10,1... | collective-permute-start | bytes 36872 | tf_op jit(solution)/shard_map/ppermute | solution.py:232
  79.0 0.2 stack.199
  79.1 0.6 bitcast_bitcast_fusion.dw_ref
  79.8 56.2 %shard_map.102 = (bf16[256,1024]{1,0:T(8,128)(2,1)}, bf16[256,1024]{1,0:T(8,128)(2,1)}, f32[2,64,128]{2,1,0:T(8,128)}) custom-call(bf16[256,256]{1,0:T(8,128)(2,1)} %copy-done.6, bf16[256,1024]{1,0:T(8,128)(2,1)} %copy-done.2, bf16[256,256]{1,0:T(8,128)(2,1)} %copy-done.7, bf16[256,1024]{1,0:T(8,128)(2,1)} %copy-done.1, f32[2,64,128]{2,1,0:T(8,128)} %bitcast_bitcast_fusion.dw_ref), custom_call_target="tpu_custom_call" | custom-call | tf_op jit(solution)/shard_map/pallas_call | solution.py:185
  135.9 2.2 %convert_multiply_fusion.49 = f32[256,1024]{1,0:T(8,128)} fusion(bf16[256,1024]{1,0:T(8,128)(2,1)} %get-tuple-element.7), kind=kLoop, calls=%fused_computation.63 | loop fusion | flops 524288 | bytes 1572864 | tf_op jit(solution)/shard_map/div | solution.py:325
  138.1 0.1 multiply_bitcast_fusion
  138.3 1.3 copy.21
  139.6 0.1 pad_maximum_fusion.1
  139.7 2.0 %collective-permute-start.7 = (bf16[2,3,38,256]{3,2,1,0:T(8,128)(2,1)S(1)}, bf16[2,3,38,256]{3,2,1,0:T(8,128)(2,1)S(1)}, u32[]{:S(2)}, u32[]{:S(2)}) collective-permute-start(bf16[2,3,38,256]{3,2,1,0:T(8,128)(2,1)S(1)} %get-tuple-element.77), channel_id=1, source_target_pairs={{32,0},{64,32},{96,64},{128,96},{160,128},{192,160},{224,192},{256... | collective-permute-start | bytes 350216 | tf_op jit(solution)/shard_map/ppermute | solution.py:235
  141.7 3.5 %collective-permute-start.6 = (bf16[2,3,38,256]{3,2,1,0:T(8,128)(2,1)S(1)}, bf16[2,3,38,256]{3,2,1,0:T(8,128)(2,1)S(1)}, u32[]{:S(2)}, u32[]{:S(2)}) collective-permute-start(bf16[2,3,38,256]{3,2,1,0:T(8,128)(2,1)S(1)} %get-tuple-element.76), channel_id=1, source_target_pairs={{0,32},{32,64},{64,96},{96,128},{128,160},{160,192},{192,224},{224... | collective-permute-start | bytes 350216 | tf_op jit(solution)/shard_map/ppermute | solution.py:232
  145.3 0.7 div.45
  146.0 1.1 collective-permute-done.6
  147.3 0.1 maximum_convert_fusion.1
  147.4 0.4 copy-done.13
  147.8 0.0 copy-done.19
  147.9 0.0 copy-done.51
  147.9 0.1 copy-done.11
  148.0 2.4 %fusion.59 = bf16[2,4,32,256]{3,2,1,0:T(8,128)(2,1)} fusion(f32[2,4,32,256]{3,2,1,0:T(8,128)S(1)} %bitcast.188, f32[2,10,38,256]{3,2,1,0:T(8,128)S(1)} %maximum_convert_fusion.1, f32[256]{0:T(256)S(1)} %bitcast.286, f32[256]{0:T(256)S(1)} %bitcast.288, f32[256]{0:T(256)S(1)} %bitcast.194, f32[256]{0:T(256)S(1)} %bitcast.196, f32[256]{0:T(256)S(1)} %bitcast.198, ...), kind=kLoop, calls=%fused_computation.119 | loop fusion | flops 6488064 | bytes 13288448 | tf_op jit(solution)/shard_map/convert_element_type | solution.py:306
  (129 shorter events, 0.5 us)
Async XLA Ops:
  0.6 58.1 %copy-start = (bf16[256,1024]{1,0:T(8,128)(2,1)S(1)}, bf16[256,1024]{1,0:T(8,128)(2,1)}, u32[]{:S(2)}) copy-start(bf16[256,1024]{1,0:T(8,128)(2,1)} %param.11) | copy-start | bytes 1572868
  2.4 14.2 %copy-start.3 = (bf16[2,4,32,256]{3,2,1,0:T(8,128)(2,1)S(1)}, bf16[2,4,32,256]{3,2,1,0:T(8,128)(2,1)}, u32[]{:S(2)}) copy-start(bf16[2,4,32,256]{3,2,1,0:T(8,128)(2,1)} %param.7) | copy-start | bytes 393220
  2.4 57.8 %all-to-all-start = ((bf16[2,64,2,256]{3,2,0,1:T(2,128)(2,1)}), bf16[2,64,2,256]{3,2,0,1:T(2,128)(2,1)S(1)}, u32[]{:S(2)}, u32[]{:S(2)}) async-start(bf16[2,64,2,256]{3,2,0,1:T(2,128)(2,1)} %copy.17), calls=%async_computation | async-start | bytes 262144 | tf_op jit(solution)/shard_map/all_to_all | solution.py:288
  16.5 14.6 %copy-start.9 = (f32[7,7,256]{2,1,0:T(8,128)S(1)}, f32[7,7,256]{2,1,0:T(8,128)}, u32[]{:S(2)}) copy-start(f32[7,7,256]{2,1,0:T(8,128)} %param.9) | copy-start | bytes 150532
  16.6 14.7 %collective-permute-start.1 = (bf16[2,4,3,256]{3,2,1,0:T(4,128)(2,1)S(1)}, bf16[2,4,3,256]{3,2,1,0:T(4,128)(2,1)S(1)}, u32[]{:S(2)}, u32[]{:S(2)}) collective-permute-start(bf16[2,4,3,256]{3,2,1,0:T(4,128)(2,1)S(1)} %get-tuple-element.83), channel_id=1, source_target_pairs={{1,0},{2,1},{3,2},{4,3},{5,4},{6,5},{7,6},{8,7},{9,8},{10,9},{11,1... | collective-permute-start | bytes 36872 | tf_op jit(solution)/shard_map/ppermute | solution.py:235
  29.2 17.9 %collective-permute-start = (bf16[2,4,3,256]{3,2,1,0:T(4,128)(2,1)S(1)}, bf16[2,4,3,256]{3,2,1,0:T(4,128)(2,1)S(1)}, u32[]{:S(2)}, u32[]{:S(2)}) collective-permute-start(bf16[2,4,3,256]{3,2,1,0:T(4,128)(2,1)S(1)} %get-tuple-element.82), channel_id=1, source_target_pairs={{0,1},{1,2},{2,3},{3,4},{4,5},{5,6},{6,7},{7,8},{8,9},{9,10},{10,1... | collective-permute-start | bytes 36872 | tf_op jit(solution)/shard_map/ppermute | solution.py:232
  31.1 24.3 %copy-start.10 = (f32[1,1,256]{2,1,0:T(1,128)}, f32[1,1,256]{2,1,0:T(1,128)S(1)}, u32[]{:S(2)}) copy-start(f32[1,1,256]{2,1,0:T(1,128)S(1)} %get-tuple-element.110) | copy-start | bytes 3076
  31.2 24.3 %copy-start.12 = (f32[1,1,256]{2,1,0:T(1,128)}, f32[1,1,256]{2,1,0:T(1,128)S(1)}, u32[]{:S(2)}) copy-start(f32[1,1,256]{2,1,0:T(1,128)S(1)} %get-tuple-element.111) | copy-start | bytes 3076
  31.2 24.3 %copy-start.14 = (f32[1,1,256]{2,1,0:T(1,128)}, f32[1,1,256]{2,1,0:T(1,128)S(1)}, u32[]{:S(2)}) copy-start(f32[1,1,256]{2,1,0:T(1,128)S(1)} %get-tuple-element.112) | copy-start | bytes 3076
  31.2 24.3 %copy-start.16 = (f32[1,1,256]{2,1,0:T(1,128)}, f32[1,1,256]{2,1,0:T(1,128)S(1)}, u32[]{:S(2)}) copy-start(f32[1,1,256]{2,1,0:T(1,128)S(1)} %get-tuple-element.113) | copy-start | bytes 3076
  31.2 24.3 %copy-start.18 = (f32[1,1,256]{2,1,0:T(1,128)}, f32[1,1,256]{2,1,0:T(1,128)S(1)}, u32[]{:S(2)}) copy-start(f32[1,1,256]{2,1,0:T(1,128)S(1)} %get-tuple-element.114) | copy-start | bytes 3076
  31.2 24.3 %copy-start.20 = (f32[1,1,256]{2,1,0:T(1,128)}, f32[1,1,256]{2,1,0:T(1,128)S(1)}, u32[]{:S(2)}) copy-start(f32[1,1,256]{2,1,0:T(1,128)S(1)} %get-tuple-element.115) | copy-start | bytes 3076
  31.2 24.3 %copy-start.22 = (f32[1,1,256]{2,1,0:T(1,128)}, f32[1,1,256]{2,1,0:T(1,128)S(1)}, u32[]{:S(2)}) copy-start(f32[1,1,256]{2,1,0:T(1,128)S(1)} %get-tuple-element.116) | copy-start | bytes 3076
  31.2 24.3 %copy-start.24 = (f32[1,1,256]{2,1,0:T(1,128)}, f32[1,1,256]{2,1,0:T(1,128)S(1)}, u32[]{:S(2)}) copy-start(f32[1,1,256]{2,1,0:T(1,128)S(1)} %get-tuple-element.117) | copy-start | bytes 3076
  31.2 24.3 %copy-start.26 = (f32[1,1,256]{2,1,0:T(1,128)}, f32[1,1,256]{2,1,0:T(1,128)S(1)}, u32[]{:S(2)}) copy-start(f32[1,1,256]{2,1,0:T(1,128)S(1)} %get-tuple-element.118) | copy-start | bytes 3076
  31.2 24.3 %copy-start.28 = (f32[1,1,256]{2,1,0:T(1,128)}, f32[1,1,256]{2,1,0:T(1,128)S(1)}, u32[]{:S(2)}) copy-start(f32[1,1,256]{2,1,0:T(1,128)S(1)} %get-tuple-element.119) | copy-start | bytes 3076
  31.2 24.3 %copy-start.30 = (f32[1,1,256]{2,1,0:T(1,128)}, f32[1,1,256]{2,1,0:T(1,128)S(1)}, u32[]{:S(2)}) copy-start(f32[1,1,256]{2,1,0:T(1,128)S(1)} %get-tuple-element.120) | copy-start | bytes 3076
  31.3 24.3 %copy-start.32 = (f32[1,1,256]{2,1,0:T(1,128)}, f32[1,1,256]{2,1,0:T(1,128)S(1)}, u32[]{:S(2)}) copy-start(f32[1,1,256]{2,1,0:T(1,128)S(1)} %get-tuple-element.121) | copy-start | bytes 3076
  47.1 7.0 %collective-permute-start.3 = (bf16[2,3,38,256]{3,2,1,0:T(8,128)(2,1)S(1)}, bf16[2,3,38,256]{3,2,1,0:T(8,128)(2,1)S(1)}, u32[]{:S(2)}, u32[]{:S(2)}) collective-permute-start(bf16[2,3,38,256]{3,2,1,0:T(8,128)(2,1)S(1)} %get-tuple-element.79), channel_id=1, source_target_pairs={{32,0},{64,32},{96,64},{128,96},{160,128},{192,160},{224,192},{256... | collective-permute-start | bytes 350216 | tf_op jit(solution)/shard_map/ppermute | solution.py:235
  50.1 5.3 %collective-permute-start.2 = (bf16[2,3,38,256]{3,2,1,0:T(8,128)(2,1)S(1)}, bf16[2,3,38,256]{3,2,1,0:T(8,128)(2,1)S(1)}, u32[]{:S(2)}, u32[]{:S(2)}) collective-permute-start(bf16[2,3,38,256]{3,2,1,0:T(8,128)(2,1)S(1)} %get-tuple-element.78), channel_id=1, source_target_pairs={{0,32},{32,64},{64,96},{96,128},{128,160},{160,192},{192,224},{224... | collective-permute-start | bytes 350216 | tf_op jit(solution)/shard_map/ppermute | solution.py:232
  53.6 2.0 %copy-start.34 = (f32[1,1,256]{2,1,0:T(1,128)}, f32[1,1,256]{2,1,0:T(1,128)S(1)}, u32[]{:S(2)}) copy-start(f32[1,1,256]{2,1,0:T(1,128)S(1)} %get-tuple-element.122) | copy-start | bytes 3076
  53.6 2.0 %copy-start.36 = (f32[1,1,256]{2,1,0:T(1,128)}, f32[1,1,256]{2,1,0:T(1,128)S(1)}, u32[]{:S(2)}) copy-start(f32[1,1,256]{2,1,0:T(1,128)S(1)} %get-tuple-element.123) | copy-start | bytes 3076
  53.6 2.0 %copy-start.38 = (f32[1,1,256]{2,1,0:T(1,128)}, f32[1,1,256]{2,1,0:T(1,128)S(1)}, u32[]{:S(2)}) copy-start(f32[1,1,256]{2,1,0:T(1,128)S(1)} %get-tuple-element.124) | copy-start | bytes 3076
  53.6 2.0 %copy-start.40 = (f32[1,1,256]{2,1,0:T(1,128)}, f32[1,1,256]{2,1,0:T(1,128)S(1)}, u32[]{:S(2)}) copy-start(f32[1,1,256]{2,1,0:T(1,128)S(1)} %get-tuple-element.125) | copy-start | bytes 3076
  53.6 2.0 %copy-start.42 = (f32[1,1,256]{2,1,0:T(1,128)}, f32[1,1,256]{2,1,0:T(1,128)S(1)}, u32[]{:S(2)}) copy-start(f32[1,1,256]{2,1,0:T(1,128)S(1)} %get-tuple-element.126) | copy-start | bytes 3076
  53.6 2.0 %copy-start.44 = (f32[1,1,256]{2,1,0:T(1,128)}, f32[1,1,256]{2,1,0:T(1,128)S(1)}, u32[]{:S(2)}) copy-start(f32[1,1,256]{2,1,0:T(1,128)S(1)} %get-tuple-element.127) | copy-start | bytes 3076
  53.6 2.0 %copy-start.46 = (f32[1,1,256]{2,1,0:T(1,128)}, f32[1,1,256]{2,1,0:T(1,128)S(1)}, u32[]{:S(2)}) copy-start(f32[1,1,256]{2,1,0:T(1,128)S(1)} %get-tuple-element.128) | copy-start | bytes 3076
  53.7 2.0 %copy-start.48 = (f32[1,1,256]{2,1,0:T(1,128)}, f32[1,1,256]{2,1,0:T(1,128)S(1)}, u32[]{:S(2)}) copy-start(f32[1,1,256]{2,1,0:T(1,128)S(1)} %get-tuple-element.129) | copy-start | bytes 3076
  53.7 2.0 %copy-start.50 = (f32[1,1,256]{2,1,0:T(1,128)}, f32[1,1,256]{2,1,0:T(1,128)S(1)}, u32[]{:S(2)}) copy-start(f32[1,1,256]{2,1,0:T(1,128)S(1)} %get-tuple-element.130) | copy-start | bytes 3076
  53.7 2.0 %copy-start.52 = (f32[1,1,256]{2,1,0:T(1,128)}, f32[1,1,256]{2,1,0:T(1,128)S(1)}, u32[]{:S(2)}) copy-start(f32[1,1,256]{2,1,0:T(1,128)S(1)} %get-tuple-element.131) | copy-start | bytes 3076
  53.7 2.0 %copy-start.54 = (f32[1,1,256]{2,1,0:T(1,128)}, f32[1,1,256]{2,1,0:T(1,128)S(1)}, u32[]{:S(2)}) copy-start(f32[1,1,256]{2,1,0:T(1,128)S(1)} %get-tuple-element.132) | copy-start | bytes 3076
  57.9 0.7 copy-start.56
  58.7 1.4 copy-start.6
  60.1 1.5 %copy-start.1 = (bf16[256,1024]{1,0:T(8,128)(2,1)}, bf16[256,1024]{1,0:T(8,128)(2,1)S(1)}, u32[]{:S(2)}) copy-start(bf16[256,1024]{1,0:T(8,128)(2,1)S(1)} %get-tuple-element.133.right_b) | copy-start | bytes 1572868
  60.1 1.2 copy-start.4
  60.4 0.9 copy-start.58
  60.4 1.3 copy-start.59
  61.7 0.9 copy-start.7
  61.7 0.8 copy-start.57
  62.5 0.8 copy-start.2
  65.0 74.6 %collective-permute-start.5 = (bf16[2,4,3,256]{3,2,1,0:T(4,128)(2,1)S(1)}, bf16[2,4,3,256]{3,2,1,0:T(4,128)(2,1)S(1)}, u32[]{:S(2)}, u32[]{:S(2)}) collective-permute-start(bf16[2,4,3,256]{3,2,1,0:T(4,128)(2,1)S(1)} %get-tuple-element.81), channel_id=1, source_target_pairs={{1,0},{2,1},{3,2},{4,3},{5,4},{6,5},{7,6},{8,7},{9,8},{10,9},{11,1... | collective-permute-start | bytes 36872 | tf_op jit(solution)/shard_map/ppermute | solution.py:235
  66.9 72.7 %collective-permute-start.4 = (bf16[2,4,3,256]{3,2,1,0:T(4,128)(2,1)S(1)}, bf16[2,4,3,256]{3,2,1,0:T(4,128)(2,1)S(1)}, u32[]{:S(2)}, u32[]{:S(2)}) collective-permute-start(bf16[2,4,3,256]{3,2,1,0:T(4,128)(2,1)S(1)} %get-tuple-element.80), channel_id=1, source_target_pairs={{0,1},{1,2},{2,3},{3,4},{4,5},{5,6},{6,7},{7,8},{8,9},{9,10},{10,1... | collective-permute-start | bytes 36872 | tf_op jit(solution)/shard_map/ppermute | solution.py:232
  135.9 2.2 %copy-start.5 = (bf16[256,1024]{1,0:T(8,128)(2,1)S(1)}, bf16[256,1024]{1,0:T(8,128)(2,1)}, u32[]{:S(2)}) copy-start(bf16[256,1024]{1,0:T(8,128)(2,1)} %get-tuple-element.8) | copy-start | bytes 1572868
  139.6 5.6 %copy-start.8 = (f32[2,64,128]{2,1,0:T(8,128)S(1)}, f32[2,64,128]{2,1,0:T(8,128)}, u32[]{:S(2)}) copy-start(f32[2,64,128]{2,1,0:T(8,128)} %get-tuple-element.9) | copy-start | bytes 196612
  139.7 6.3 %collective-permute-start.7 = (bf16[2,3,38,256]{3,2,1,0:T(8,128)(2,1)S(1)}, bf16[2,3,38,256]{3,2,1,0:T(8,128)(2,1)S(1)}, u32[]{:S(2)}, u32[]{:S(2)}) collective-permute-start(bf16[2,3,38,256]{3,2,1,0:T(8,128)(2,1)S(1)} %get-tuple-element.77), channel_id=1, source_target_pairs={{32,0},{64,32},{96,64},{128,96},{160,128},{192,160},{224,192},{256... | collective-permute-start | bytes 350216 | tf_op jit(solution)/shard_map/ppermute | solution.py:235
  141.7 5.4 %collective-permute-start.6 = (bf16[2,3,38,256]{3,2,1,0:T(8,128)(2,1)S(1)}, bf16[2,3,38,256]{3,2,1,0:T(8,128)(2,1)S(1)}, u32[]{:S(2)}, u32[]{:S(2)}) collective-permute-start(bf16[2,3,38,256]{3,2,1,0:T(8,128)(2,1)S(1)} %get-tuple-element.76), channel_id=1, source_target_pairs={{0,32},{32,64},{64,96},{96,128},{128,160},{160,192},{192,224},{224... | collective-permute-start | bytes 350216 | tf_op jit(solution)/shard_map/ppermute | solution.py:232
  147.1 0.7 copy-start.19
  147.1 0.7 copy-start.21
  (21 other events, 14.0 us)

commit v2 on v1

--- a/solution.py
+++ b/solution.py
@@ -10,16 +10,174 @@
 norm_eps = 1e-06
 MESH = pl.DeviceIdType.MESH
 
+def start_remote(source, target, ssem, rsem, device_to):
+    copy = pltpu.make_async_remote_copy(
+        src_ref=source, dst_ref=target, send_sem=ssem, recv_sem=rsem,
+        device_id=device_to, device_id_type=MESH,
+    )
+    copy.start()
+    return copy
+
+
+DIRECTIONS = [(0, 1), (0, -1), (1, 1), (1, -1), (-1, 1), (-1, -1), (1, 0), (-1, 0)]
+WIDTH = 3
+
+
+def halo_friends(lat, lon, lats, lons):
+    return [
+        {"lat": lax.rem(lat + dl + lats, lats), "lon": lax.rem(lon + dn + lons, lons)}
+        for dl, dn in DIRECTIONS
+    ]
+
+
+def halo_copies(block, edges, low, high, left, right, ssem, rsem):
+    lats, lons = lax.axis_size("lat"), lax.axis_size("lon")
+    lat, lon = lax.axis_index("lat"), lax.axis_index("lon")
+    rows = block.shape[1]
+    copies = []
+    for k, (dl, dn) in enumerate(DIRECTIONS):
+        if dl == 0:
+            src_rows, dst_rows = pl.ds(0, rows), pl.ds(WIDTH, rows)
+        elif dl > 0:
+            src_rows, dst_rows = pl.ds(rows - WIDTH, WIDTH), pl.ds(0, WIDTH)
+        else:
+            src_rows, dst_rows = pl.ds(0, WIDTH), pl.ds(WIDTH + rows, WIDTH)
+        if dn == 0:
+            source, target = block.at[:, src_rows], (low if dl > 0 else high)
+        elif dn > 0:
+            source, target = edges.at[1, src_rows], left.at[dst_rows]
+        else:
+            source, target = edges.at[0, src_rows], right.at[dst_rows]
+        copy = pltpu.make_async_remote_copy(
+            src_ref=source, dst_ref=target, send_sem=ssem.at[k], recv_sem=rsem.at[k],
+            device_id={
+                "lat": jnp.clip(lat + dl, 0, lats - 1),
+                "lon": lax.rem(lon + dn + lons, lons),
+            },
+            device_id_type=MESH,
+        )
+        if dl == 0:
+            sends = comes = None
+        elif dl > 0:
+            sends, comes = lat < lats - 1, lat > 0
+        else:
+            sends, comes = lat > 0, lat < lats - 1
+        copies.append((copy, sends, comes))
+    return copies
+
+
+def run_if(condition, action):
+    if condition is None:
+        action()
+    else:
+        pl.when(condition)(action)
+
+
+def halo_start(copies, low, high, left, right):
+    lats, lat = lax.axis_size("lat"), lax.axis_index("lat")
+    for copy, sends, _ in copies:
+        run_if(sends, copy.start)
+    rows = left.shape[0]
+
+    @pl.when(lat == 0)
+    def _():
+        low[...] = jnp.zeros_like(low)
+        left[:WIDTH] = jnp.zeros((WIDTH,) + left.shape[1:], left.dtype)
+        right[:WIDTH] = jnp.zeros((WIDTH,) + right.shape[1:], right.dtype)
+
+    @pl.when(lat == lats - 1)
+    def _():
+        high[...] = jnp.zeros_like(high)
+        left[rows - WIDTH :] = jnp.zeros((WIDTH,) + left.shape[1:], left.dtype)
+        right[rows - WIDTH :] = jnp.zeros((WIDTH,) + right.shape[1:], right.dtype)
+
+
+def halo_wait(copies):
+    for copy, sends, comes in copies:
+        run_if(sends, copy.wait_send)
+        run_if(comes, copy.wait_recv)
+
+
+def halo_shapes(block):
+    batch, rows, cols, channels = block.shape
+    across = jax.ShapeDtypeStruct((batch, WIDTH, cols, channels), block.dtype)
+    along = jax.ShapeDtypeStruct((rows + 2 * WIDTH, batch * WIDTH, channels), block.dtype)
+    return (across, across, along, along)
+
+
+def pack_edges(block):
+    batch, rows, cols, channels = block.shape
+    sides = jnp.stack([block[:, :, :WIDTH], block[:, :, cols - WIDTH :]])
+    return sides.transpose(0, 2, 1, 3, 4).reshape(2, rows, batch * WIDTH, channels)
+
+
+def join_halo(block, low, high, left, right):
+    batch, rows, cols, channels = block.shape
+
+    def columns(side):
+        return side.reshape(rows + 2 * WIDTH, batch, WIDTH, channels).transpose(1, 0, 2, 3)
+
+    middle = jnp.concatenate([low, block, high], axis=1)
+    return jnp.concatenate([columns(left), middle, columns(right)], axis=2)
+
+
+def front_kernel(
+    block, edges, sent, low, high, left, right, came, halo_ssem, halo_rsem, ssem, rsem, local_sem
+):
+    lats, lons = lax.axis_size("lat"), lax.axis_size("lon")
+    lat, lon = lax.axis_index("lat"), lax.axis_index("lon")
+    peers = [lax.rem(lat + d, lats) for d in range(lats)]
+    friends = halo_friends(lat, lon, lats, lons)[:6] + [{"lat": p, "lon": lon} for p in peers[1:]]
+    barrier = pltpu.get_barrier_semaphore()
+    for friend in friends:
+        pl.semaphore_signal(barrier, inc=1, device_id=friend, device_id_type=MESH)
+    mine = pltpu.make_async_copy(sent.at[lat], came.at[lat], local_sem)
+    mine.start()
+    pl.semaphore_wait(barrier, len(friends))
+    halo = halo_copies(block, edges, low, high, left, right, halo_ssem, halo_rsem)
+    halo_start(halo, low, high, left, right)
+    copies = [
+        start_remote(
+            sent.at[peers[d]], came.at[lat], ssem.at[d], rsem.at[d], {"lat": peers[d], "lon": lon}
+        )
+        for d in range(1, lats)
+    ]
+    halo_wait(halo)
+    mine.wait()
+    for copy in copies:
+        copy.wait()
+
+
+def front_exchange(block, edges, sent):
+    vmem = pl.BlockSpec(memory_space=pltpu.VMEM)
+    lats = sent.shape[0]
+    return pl.pallas_call(
+        front_kernel,
+        out_shape=halo_shapes(block) + (jax.ShapeDtypeStruct(sent.shape, sent.dtype),),
+        in_specs=[vmem] * 3,
+        out_specs=(vmem,) * 5,
+        scratch_shapes=[
+            pltpu.SemaphoreType.DMA((8,)),
+            pltpu.SemaphoreType.DMA((8,)),
+            pltpu.SemaphoreType.DMA((lats,)),
+            pltpu.SemaphoreType.DMA((lats,)),
+            pltpu.SemaphoreType.DMA,
+        ],
+        compiler_params=pltpu.CompilerParams(collective_id=1, has_side_effects=True),
+    )(block, edges, sent)
+
+
 BLOCKS, SIDE, SPLIT, TILE, DW_ROWS, DW_PAD = 16, 128, 64, 8, 4, 16
 LOWER = SIDE - SPLIT + DW_PAD
 CHIPS_Z = 16
 
 
 def sum_kernel(
-    left_a, right_a, left_b, right_b, dw_ref, out_a, out_b, out_dw,
+    left_a, right_a, left_b, right_b, dw_ref, block_ref, edges,
+    out_a, out_b, out_dw, halo_low, halo_high, halo_left, halo_right,
     own, other, dw_other, top, low, top_in1, low_in1, top1, low1, top_in2, low_in2,
     z_send, z_in, z_own, z_all, top_g1, low_g1, top_all, low_all,
-    core_ssem, core_rsem, xy_ssem, xy_rsem, z_ssem, z_rsem,
+    core_ssem, core_rsem, xy_ssem, xy_rsem, z_ssem, z_rsem, halo_ssem, halo_rsem,
 ):
     lat, lon = lax.axis_index("lat"), lax.axis_index("lon")
     core = lax.rem(lat, 2)
@@ -43,16 +201,9 @@
 
     barrier = pltpu.get_barrier_semaphore()
     friends = [partner] + x_devices[1:] + y_devices[1:] + z_devices[1:]
+    friends = friends + halo_friends(lat, lon, lax.axis_size("lat"), lax.axis_size("lon"))
     for friend in friends:
         pl.semaphore_signal(barrier, inc=1, device_id=friend, device_id_type=MESH)
-
-    def send(source, target, ssem, rsem, device_to):
-        copy = pltpu.make_async_remote_copy(
-            src_ref=source, dst_ref=target, send_sem=ssem, recv_sem=rsem,
-            device_id=device_to, device_id_type=MESH,
-        )
-        copy.start()
-        return copy
 
     for which, (left, right) in enumerate(((left_a, right_a), (left_b, right_b))):
         product = lax.dot_general(
@@ -63,9 +214,13 @@
             own[which, block] = product[row : row + SIDE, col : col + SIDE]
     pl.semaphore_wait(barrier, len(friends))
 
+    halo = halo_copies(
+        block_ref, edges, halo_low, halo_high, halo_left, halo_right, halo_ssem, halo_rsem
+    )
+    halo_start(halo, halo_low, halo_high, halo_left, halo_right)
     copies = [
-        send(own.at[1 - core], other, core_ssem.at[0], core_rsem.at[0], partner),
-        send(dw_ref.at[1 - core], dw_other, core_ssem.at[1], core_rsem.at[1], partner),
+        start_remote(own.at[1 - core], other, core_ssem.at[0], core_rsem.at[0], partner),
+        start_remote(dw_ref.at[1 - core], dw_other, core_ssem.at[1], core_rsem.at[1], partner),
     ]
     for copy in copies:
         copy.wait()
@@ -82,10 +237,10 @@
     copies = []
     for d in (2, 1, 3):
         copies.append(
-            send(top.at[x_peers[d]], top_in1.at[d], xy_ssem.at[0, d], xy_rsem.at[0, d], x_devices[d])
-        )
-        copies.append(
-            send(low.at[y_peers[d]], low_in1.at[d], xy_ssem.at[1, d], xy_rsem.at[1, d], y_devices[d])
+            start_remote(top.at[x_peers[d]], top_in1.at[d], xy_ssem.at[0, d], xy_rsem.at[0, d], x_devices[d])
+        )
+        copies.append(
+            start_remote(low.at[y_peers[d]], low_in1.at[d], xy_ssem.at[1, d], xy_rsem.at[1, d], y_devices[d])
         )
     for copy in copies:
         copy.wait()
@@ -95,10 +250,10 @@
     copies = []
     for d in (2, 1, 3):
         copies.append(
-            send(top1.at[y_peers[d]], top_in2.at[d], xy_ssem.at[2, d], xy_rsem.at[2, d], y_devices[d])
-        )
-        copies.append(
-            send(low1.at[x_peers[d]], low_in2.at[d], xy_ssem.at[3, d], xy_rsem.at[3, d], x_devices[d])
+            start_remote(top1.at[y_peers[d]], top_in2.at[d], xy_ssem.at[2, d], xy_rsem.at[2, d], y_devices[d])
+        )
+        copies.append(
+            start_remote(low1.at[x_peers[d]], low_in2.at[d], xy_ssem.at[3, d], xy_rsem.at[3, d], x_devices[d])
         )
     for copy in copies:
         copy.wait()
@@ -113,7 +268,7 @@
     copies = []
     for d in order:
         copies.append(
-            send(z_send.at[z_peers[d]], z_in.at[z], z_ssem.at[0, d], z_rsem.at[0, d], z_devices[d])
+            start_remote(z_send.at[z_peers[d]], z_in.at[z], z_ssem.at[0, d], z_rsem.at[0, d], z_devices[d])
         )
     z_in[z] = z_send[z]
     for copy in copies:
@@ -126,7 +281,7 @@
     copies = []
     for d in order:
         copies.append(
-            send(z_own.at[:TILE], z_all.at[z], z_ssem.at[1, d], z_rsem.at[1, d], z_devices[d])
+            start_remote(z_own.at[:TILE], z_all.at[z], z_ssem.at[1, d], z_rsem.at[1, d], z_devices[d])
         )
     z_all[z] = z_own[:TILE]
     for copy in copies:
@@ -141,10 +296,10 @@
     copies = []
     for d in (2, 1, 3):
         copies.append(
-            send(top_g1.at[y], top_g1.at[y], xy_ssem.at[4, d], xy_rsem.at[4, d], y_devices[d])
-        )
-        copies.append(
-            send(low_g1.at[x], low_g1.at[x], xy_ssem.at[5, d], xy_rsem.at[5, d], x_devices[d])
+            start_remote(top_g1.at[y], top_g1.at[y], xy_ssem.at[4, d], xy_rsem.at[4, d], y_devices[d])
+        )
+        copies.append(
+            start_remote(low_g1.at[x], low_g1.at[x], xy_ssem.at[5, d], xy_rsem.at[5, d], x_devices[d])
         )
     for copy in copies:
         copy.wait()
@@ -152,10 +307,10 @@
     copies = []
     for d in (2, 1, 3):
         copies.append(
-            send(top_g1, top_all.at[core, x], xy_ssem.at[6, d], xy_rsem.at[6, d], x_devices[d])
-        )
-        copies.append(
-            send(low_g1, low_all.at[core, y], xy_ssem.at[7, d], xy_rsem.at[7, d], y_devices[d])
+            start_remote(top_g1, top_all.at[core, x], xy_ssem.at[6, d], xy_rsem.at[6, d], x_devices[d])
+        )
+        copies.append(
+            start_remote(low_g1, low_all.at[core, y], xy_ssem.at[7, d], xy_rsem.at[7, d], y_devices[d])
         )
     top_all[core, x] = top_g1[...]
     low_all[core, y] = low_g1[...]
@@ -163,8 +318,8 @@
         copy.wait()
 
     copies = [
-        send(top_all.at[core], top_all.at[core], core_ssem.at[2], core_rsem.at[2], partner),
-        send(low_all.at[core], low_all.at[core], core_ssem.at[3], core_rsem.at[3], partner),
+        start_remote(top_all.at[core], top_all.at[core], core_ssem.at[2], core_rsem.at[2], partner),
+        start_remote(low_all.at[core], low_all.at[core], core_ssem.at[3], core_rsem.at[3], partner),
     ]
     for copy in copies:
         copy.wait()
@@ -176,9 +331,10 @@
             out[row + SPLIT : row + SIDE, col : col + SIDE] = low_all[which, by, bx, : SIDE - SPLIT]
             dw_rows = low_all[which, by, bx, SIDE - SPLIT :].astype(jnp.float32)[:DW_ROWS]
             out_dw[which, DW_ROWS * block : DW_ROWS * (block + 1)] = dw_rows
-
-
-def sum_gradients(left_a, right_a, left_b, right_b, dw):
+    halo_wait(halo)
+
+
+def sum_gradients(left_a, right_a, left_b, right_b, dw, grid, edges):
     f32, bf16 = jnp.float32, jnp.bfloat16
     vmem = pl.BlockSpec(memory_space=pltpu.VMEM)
     shape = (left_a.shape[1], right_a.shape[1])
@@ -188,9 +344,10 @@
             jax.ShapeDtypeStruct(shape, bf16),
             jax.ShapeDtypeStruct(shape, bf16),
             jax.ShapeDtypeStruct(dw.shape, f32),
-        ),
-        in_specs=[vmem] * 5,
-        out_specs=(vmem,) * 3,
+        )
+        + halo_shapes(grid),
+        in_specs=[vmem] * 7,
+        out_specs=(vmem,) * 7,
         scratch_shapes=[
             pltpu.VMEM((2, BLOCKS, SIDE, SIDE), f32),
             pltpu.VMEM((BLOCKS, SIDE, SIDE), f32),
@@ -217,24 +374,11 @@
             pltpu.SemaphoreType.DMA((8, 4)),
             pltpu.SemaphoreType.DMA((2, CHIPS_Z)),
             pltpu.SemaphoreType.DMA((2, CHIPS_Z)),
+            pltpu.SemaphoreType.DMA((8,)),
+            pltpu.SemaphoreType.DMA((8,)),
         ],
         compiler_params=pltpu.CompilerParams(collective_id=0, has_side_effects=True),
-    )(left_a, right_a, left_b, right_b, dw)
-
-
-def with_halo(block, sides, width, periodic):
-    for axis, dim in sides:
-        count = lax.axis_size(axis)
-        forward = [(i, i + 1) for i in range(count - 1)]
-        if periodic:
-            forward.append((count - 1, 0))
-        backward = [(target, source) for source, target in forward]
-        low = lax.ppermute(
-            lax.slice_in_dim(block, block.shape[dim] - width, None, axis=dim), axis, forward
-        )
-        high = lax.ppermute(lax.slice_in_dim(block, 0, width, axis=dim), axis, backward)
-        block = jnp.concatenate([low, block, high], axis=dim)
-    return block
+    )(left_a, right_a, left_b, right_b, dw, grid, edges)
 
 
 def gelu_tanh(values):
@@ -267,10 +411,12 @@
 def local(student, teacher, dw_weight, norm_gain, w_in, w_out, layer_scale):
     batch_size, tile_rows, tile_cols, channel_count = student.shape
     kernel_size = dw_weight.shape[0]
-    half_kernel = kernel_size // 2
     cell_total = batch_size * tile_rows * lax.axis_size("lat") * tile_cols * lax.axis_size("lon")
-    lon_padded = with_halo(student, (("lon", 2),), half_kernel, True)
-    padded_bf = with_halo(lon_padded, (("lat", 1),), half_kernel, False)
+    lats = lax.axis_size("lat")
+    sent = teacher.reshape(batch_size, lats, -1, teacher.shape[2], channel_count)
+    sent = sent.transpose(1, 0, 2, 3, 4).reshape(lats, -1, channel_count)
+    *halo, came = front_exchange(student, pack_edges(student), sent)
+    padded_bf = join_halo(student, *halo)
     padded = padded_bf.astype(jnp.float32)
     smoothed = apply_stencil(padded, dw_weight, tile_rows, tile_cols, False).reshape(
         -1, channel_count
@@ -285,7 +431,8 @@
     hidden = gelu_tanh(preact).astype(jnp.bfloat16)
     mlp_out = jnp.dot(hidden, w_out, preferred_element_type=jnp.float32)
     output = student.reshape(-1, channel_count).astype(jnp.float32) + layer_scale * mlp_out
-    target = lax.all_to_all(teacher, "lat", split_axis=1, concat_axis=2, tiled=True)
+    target = came.reshape(lats, batch_size, tile_rows, tile_cols // lats, channel_count)
+    target = target.transpose(1, 2, 0, 3, 4)
     misfit = output - target.reshape(-1, channel_count).astype(jnp.float32)
     out_grad = (layer_scale * misfit).astype(jnp.bfloat16)
     hidden_grad = lax.dot_general(
@@ -300,10 +447,6 @@
     second_mean = jnp.mean(unit_grad * unit_norm, axis=-1, keepdims=True)
     conv_grad = (inv_std * (unit_grad - first_mean - unit_norm * second_mean)).astype(jnp.bfloat16)
     conv_grid = conv_grad.reshape(student.shape)
-    grad_lon = with_halo(conv_grid, (("lon", 2),), half_kernel, True)
-    padded_grad = with_halo(grad_lon, (("lat", 1),), half_kernel, False).astype(jnp.float32)
-    back_conv = apply_stencil(padded_grad, dw_weight, tile_rows, tile_cols, True)
-    grad_student = (misfit.reshape(student.shape) + back_conv).astype(jnp.bfloat16)
     conv_grad_f = conv_grid.astype(jnp.float32)
     kernel_terms = []
     for row_off in range(kernel_size):
@@ -318,7 +461,12 @@
     taps = kernel_size * kernel_size
     part_dw = jnp.pad(jnp.stack(kernel_terms), ((0, BLOCKS * DW_ROWS - taps), (0, 0)))
     part_dw = part_dw.reshape(BLOCKS * DW_ROWS, 2, SIDE).transpose(1, 0, 2)
-    sum_in, sum_out, sum_dw = sum_gradients(normed, preact_grad, out_grad, hidden, part_dw)
+    sum_in, sum_out, sum_dw, *halo = sum_gradients(
+        normed, preact_grad, out_grad, hidden, part_dw, conv_grid, pack_edges(conv_grid)
+    )
+    padded_grad = join_halo(conv_grid, *halo).astype(jnp.float32)
+    back_conv = apply_stencil(padded_grad, dw_weight, tile_rows, tile_cols, True)
+    grad_student = (misfit.reshape(student.shape) + back_conv).astype(jnp.bfloat16)
     sum_dw = sum_dw.transpose(1, 0, 2)[:taps].reshape(kernel_size, kernel_size, channel_count)
     return (
         grad_student,

time: 151 us -> 117 us (0.77)
  starting transfers between devices: 54.6 us -> 0 us
  Pallas kernels: 56.2 us -> 92.6 us
  waiting for transfers between devices: 18.6 us -> 0 us
  local copies, waits for them, and re-layouts: 7.61 us -> 13.1 us
    ppermute x8 -> x0, starting transfers between devices: 40.5 us -> none  [the longest x4 20.9 us: with_halo(): lax.ppermute(lax.slice_in_dim(block, block.shape[dim] - width, None, axis...]
    pallas_call x0 -> x1, Pallas kernels: none -> 37 us  [front_exchange(): pl.pallas_call(front_kernel, out_shape=halo_shapes(block) + (jax.ShapeDty...]
    ppermute x8 -> x0, waiting for transfers between devices: 18.6 us -> none  [the longest x4 18.1 us: with_halo(): lax.ppermute(lax.slice_in_dim(block, block.shape[dim] - width, None, axis...]
    all_to_all x1 -> x0, starting transfers between devices: 14.2 us -> none  [local(): lax.all_to_all(teacher, 'lat', split_axis=1, concat_axis=2, tiled=True)]
    reshape x0 -> x10, local copies, waits for them, and re-layouts: none -> 3.83 us  [the longest x6 1.79 us: columns(): side.reshape(rows + 2 * WIDTH, batch, WIDTH, channels).transpose(1, 0, 2, 3)]
    unnamed x122 -> x45, local copies, waits for them, and re-layouts: 5.65 us -> 5.35 us
  transfers between devices with their start and end apart: 9 -> 0, of which waited for: 4 -> 0; matrix products, arithmetic and copies ran while one was open for 6% -> 0% of each run, Pallas kernels for 37% -> 0%
where the time goes in v2:
time: 117 us
  Pallas kernels  92.6 us (79%)
  local copies, waits for them, and re-layouts  13.1 us (11%)
  other arithmetic  7.78 us (7%)
  matrix products  2.04 us (2%)
    pallas_call x1, Pallas kernels, sum_gradients(): pl.pallas_call(sum_kernel, out_shape=(jax.ShapeDtypeStruct(shape, bf16),...  55.6 us
    pallas_call x1, Pallas kernels, front_exchange(): pl.pallas_call(front_kernel, out_shape=halo_shapes(block) + (jax.ShapeDty...  37 us
    unnamed x45, local copies, waits for them, and re-layouts  5.35 us
    convert_element_type x1, other arithmetic, local(): (misfit.reshape(student.shape) + back_conv).astype(jnp.bfloat16)  2.49 us

profile of v2, /device:TPU:1, one launch (start us, length us, event | category | flops | bytes accessed | tf_op | source)
XLA Modules:
  0.0 116.5 jit_solution(14426820266962850146)
XLA Ops:
  0.6 0.0 copy-start
  0.7 0.9 slice_bitcast_fusion.3
  1.6 0.6 copy.18.edges
  2.2 0.1 copy.38
  2.3 0.7 reshape.149.sent
  3.0 37.0 %shard_map.102 = (bf16[2,3,32,256]{3,2,1,0:T(8,128)(2,1)}, bf16[2,3,32,256]{3,2,1,0:T(8,128)(2,1)}, bf16[10,6,256]{2,1,0:T(8,128)(2,1)}, bf16[10,6,256]{2,1,0:T(8,128)(2,1)}, bf16[16,16,256]{2,1,0:T(8,128)(2,1)}) custom-call(bf16[2,4,32,256]{3,2,1,0:T(8,128)(2,1)} %block.1, bf16[2,4,6,256]{3,2,1,0:T(8,128)(2,1)} %copy.18.edges, ...), custom_call_target="tpu_custom_call" | custom-call | tf_op jit(solution)/shard_map/pallas_call | solution.py:154
  40.0 1.0 reshape.161
  41.1 0.2 reshape.160
  41.3 0.6 copy-done.19
  41.9 0.0 copy-start.5
  42.0 0.8 copy-done.13
  42.8 0.1 copy-done.5
  42.8 0.1 copy-done.12
  42.9 0.1 maximum_convert_fusion
  43.0 0.7 copy-done.17
  43.8 1.8 %fusion.109 = (f32[2,4,32]{2,1,0:T(4,128)S(1)}, f32[2,4,32,256]{3,2,1,0:T(8,128)S(1)}) fusion(f32[2,10,38,256]{3,2,1,0:T(8,128)S(1)} %maximum_convert_fusion, f32[256]{0:T(256)S(1)} %bitcast.242, f32[256]{0:T(256)S(1)} %bitcast.244, f32[256]{0:T(256)S(1)} %bitcast.248, f32[256]{0:T(256)S(1)} %bitcast.250, f32[256]{0:T(256)S(1)} %bitcast.252, ...), kind=kLoop, calls=%fused_computation.243 | loop fusion | flops 6422272 | bytes 13158400 | tf_op jit(solution)/shard_map/reduce_sum | solution.py:424
  45.6 0.2 multiply_reduce_fusion.1
  45.8 0.1 rsqrt.12
  45.9 0.1 div.35
  46.0 0.6 copy-done.20
  46.6 0.1 multiply_convert_fusion.3.left_a
  46.8 0.0 copy-start.9
  46.8 0.0 copy-start.6
  46.8 0.5 multiply_convert_fusion
  47.3 0.1 copy-done.9
  47.4 0.4 copy-done.6
  47.9 0.3 copy-done.21
  48.1 0.3 multiply_convert_fusion.2
  48.5 0.8 fusion.right_a
  49.3 0.0 copy-start.4
  49.3 0.5 fusion.108
  49.7 0.3 copy-done.4
  50.1 0.6 fusion.56
  50.7 0.4 fusion.20
  51.1 0.5 fusion.38
  51.7 0.2 stack.220
  51.8 0.6 bitcast_bitcast_fusion.dw_ref
  52.5 0.6 copy.24.edges
  53.1 55.6 %shard_map.103 = (bf16[256,1024]{1,0:T(8,128)(2,1)}, bf16[256,1024]{1,0:T(8,128)(2,1)}, f32[2,64,128]{2,1,0:T(8,128)}, bf16[2,3,32,256]{3,2,1,0:T(8,128)(2,1)}, ...) custom-call(bf16[256,256]{1,0:T(8,128)(2,1)} %copy-done.9, ...), custom_call_target="tpu_custom_call" | custom-call | tf_op jit(solution)/shard_map/pallas_call | solution.py:341
  108.8 0.8 reshape.158
  109.7 0.9 reshape.157
  110.6 0.0 copy-done.14
  110.6 0.1 maximum_convert_fusion.1
  110.8 2.5 %fusion.59 = bf16[2,4,32,256]{3,2,1,0:T(8,128)(2,1)} fusion(f32[2,4,32,256]{3,2,1,0:T(8,128)S(1)} %bitcast.216, f32[2,10,38,256]{3,2,1,0:T(8,128)S(1)} %maximum_convert_fusion.1, f32[256]{0:T(256)S(1)} %bitcast.243, f32[256]{0:T(256)S(1)} %bitcast.245, f32[256]{0:T(256)S(1)} %bitcast.249, f32[256]{0:T(256)S(1)} %bitcast.251, f32[256]{0:T(256)S(1)} %bitcast.253, ...), kind=kLoop, calls=%fused_computation.119 | loop fusion | flops 6488064 | bytes 13288448 | tf_op jit(solution)/shard_map/convert_element_type | solution.py:469
  113.3 1.1 convert_multiply_fusion.49
  114.4 0.1 multiply_bitcast_fusion
  114.5 1.3 %copy.28 = f32[1024,256]{1,0:T(8,128)} copy(f32[1024,256]{0,1:T(8,128)S(1)} %multiply_bitcast_fusion) | data formatting | bytes 2097152
  115.8 0.7 div.45
  (48 shorter events, 0.4 us)
Async XLA Ops:
  0.6 46.1 %copy-start = (bf16[256,1024]{1,0:T(8,128)(2,1)S(1)}, bf16[256,1024]{1,0:T(8,128)(2,1)}, u32[]{:S(2)}) copy-start(bf16[256,1024]{1,0:T(8,128)(2,1)} %param.11) | copy-start | bytes 1572868
  0.6 1.6 %copy-start.11 = (bf16[2,64,2,256]{3,2,1,0:T(2,128)(2,1)S(1)}, bf16[2,64,2,256]{3,2,1,0:T(2,128)(2,1)}, u32[]{:S(2)}) copy-start(bf16[2,64,2,256]{3,2,1,0:T(2,128)(2,1)} %param.8) | copy-start | bytes 393220
  41.1 0.8 copy-start.19
  41.1 0.8 copy-start.18
  41.9 0.9 copy-start.13
  41.9 0.9 copy-start.5
  41.9 0.9 copy-start.12
  42.9 0.8 copy-start.17
  45.9 0.7 copy-start.20
  46.8 0.7 copy-start.9
  46.8 1.1 copy-start.6
  47.4 1.0 copy-start.3
  47.4 0.7 copy-start.21
  48.5 0.8 copy-start.10
  49.3 0.8 copy-start.4
  50.7 1.7 %copy-start.1 = (bf16[256,256]{1,0:T(8,128)(2,1)}, bf16[256,256]{1,0:T(8,128)(2,1)S(1)}, u32[]{:S(2)}) copy-start(bf16[256,256]{1,0:T(8,128)(2,1)S(1)} %get-tuple-element.87) | copy-start | bytes 393220
  108.8 1.8 %copy-start.15 = (bf16[2,3,32,256]{3,2,1,0:T(8,128)(2,1)S(1)}, bf16[2,3,32,256]{3,2,1,0:T(8,128)(2,1)}, u32[]{:S(2)}) copy-start(bf16[2,3,32,256]{3,2,1,0:T(8,128)(2,1)} %get-tuple-element.23) | copy-start | bytes 294916
  109.6 0.9 copy-start.2
  109.7 1.0 copy-start.14
  110.8 2.5 %copy-start.8 = (bf16[256,1024]{1,0:T(8,128)(2,1)S(1)}, bf16[256,1024]{1,0:T(8,128)(2,1)}, u32[]{:S(2)}) copy-start(bf16[256,1024]{1,0:T(8,128)(2,1)} %get-tuple-element.25) | copy-start | bytes 1572868
  113.3 1.1 copy-start.7
  114.5 1.3 %copy-start.16 = (f32[2,64,128]{2,1,0:T(8,128)S(1)}, f32[2,64,128]{2,1,0:T(8,128)}, u32[]{:S(2)}) copy-start(f32[2,64,128]{2,1,0:T(8,128)} %get-tuple-element.27) | copy-start | bytes 196612

commit v3 on v2

--- a/solution.py
+++ b/solution.py
@@ -19,14 +19,14 @@
     return copy
 
 
-DIRECTIONS = [(0, 1), (0, -1), (1, 1), (1, -1), (-1, 1), (-1, -1), (1, 0), (-1, 0)]
 WIDTH = 3
 
 
 def halo_friends(lat, lon, lats, lons):
+    steps = [(0, 1), (0, -1), (1, 0), (-1, 0)]
     return [
         {"lat": lax.rem(lat + dl + lats, lats), "lon": lax.rem(lon + dn + lons, lons)}
-        for dl, dn in DIRECTIONS
+        for dl, dn in steps
     ]
 
 
@@ -34,34 +34,27 @@
     lats, lons = lax.axis_size("lat"), lax.axis_size("lon")
     lat, lon = lax.axis_index("lat"), lax.axis_index("lon")
     rows = block.shape[1]
-    copies = []
-    for k, (dl, dn) in enumerate(DIRECTIONS):
-        if dl == 0:
-            src_rows, dst_rows = pl.ds(0, rows), pl.ds(WIDTH, rows)
-        elif dl > 0:
-            src_rows, dst_rows = pl.ds(rows - WIDTH, WIDTH), pl.ds(0, WIDTH)
-        else:
-            src_rows, dst_rows = pl.ds(0, WIDTH), pl.ds(WIDTH + rows, WIDTH)
-        if dn == 0:
-            source, target = block.at[:, src_rows], (low if dl > 0 else high)
-        elif dn > 0:
-            source, target = edges.at[1, src_rows], left.at[dst_rows]
-        else:
-            source, target = edges.at[0, src_rows], right.at[dst_rows]
+    up = {"lat": jnp.minimum(lat + 1, lats - 1), "lon": lon}
+    down = {"lat": jnp.maximum(lat - 1, 0), "lon": lon}
+    first = lat == 0
+    last = lat == lats - 1
+    inner_up, inner_down = jnp.logical_not(last), jnp.logical_not(first)
+    plan = [
+        (edges.at[1], left.at[1], {"lat": lat, "lon": lax.rem(lon + 1, lons)}, None, None),
+        (edges.at[0], right.at[1], {"lat": lat, "lon": lax.rem(lon + lons - 1, lons)}, None, None),
+        (block.at[:, pl.ds(rows - WIDTH, WIDTH)], low, up, inner_up, inner_down),
+        (block.at[:, pl.ds(0, WIDTH)], high, down, inner_down, inner_up),
+        (left.at[1], left.at[0], up, inner_up, inner_down),
+        (right.at[1], right.at[0], up, inner_up, inner_down),
+        (left.at[1], left.at[2], down, inner_down, inner_up),
+        (right.at[1], right.at[2], down, inner_down, inner_up),
+    ]
+    copies = []
+    for k, (source, target, device_to, sends, comes) in enumerate(plan):
         copy = pltpu.make_async_remote_copy(
             src_ref=source, dst_ref=target, send_sem=ssem.at[k], recv_sem=rsem.at[k],
-            device_id={
-                "lat": jnp.clip(lat + dl, 0, lats - 1),
-                "lon": lax.rem(lon + dn + lons, lons),
-            },
-            device_id_type=MESH,
-        )
-        if dl == 0:
-            sends = comes = None
-        elif dl > 0:
-            sends, comes = lat < lats - 1, lat > 0
-        else:
-            sends, comes = lat > 0, lat < lats - 1
+            device_id=device_to, device_id_type=MESH,
+        )
         copies.append((copy, sends, comes))
     return copies
 
@@ -75,47 +68,55 @@
 
 def halo_start(copies, low, high, left, right):
     lats, lat = lax.axis_size("lat"), lax.axis_index("lat")
-    for copy, sends, _ in copies:
+    for copy, sends, _ in copies[:4]:
         run_if(sends, copy.start)
-    rows = left.shape[0]
 
     @pl.when(lat == 0)
     def _():
         low[...] = jnp.zeros_like(low)
-        left[:WIDTH] = jnp.zeros((WIDTH,) + left.shape[1:], left.dtype)
-        right[:WIDTH] = jnp.zeros((WIDTH,) + right.shape[1:], right.dtype)
+        left[0] = jnp.zeros(left.shape[1:], left.dtype)
+        right[0] = jnp.zeros(right.shape[1:], right.dtype)
 
     @pl.when(lat == lats - 1)
     def _():
         high[...] = jnp.zeros_like(high)
-        left[rows - WIDTH :] = jnp.zeros((WIDTH,) + left.shape[1:], left.dtype)
-        right[rows - WIDTH :] = jnp.zeros((WIDTH,) + right.shape[1:], right.dtype)
+        left[2] = jnp.zeros(left.shape[1:], left.dtype)
+        right[2] = jnp.zeros(right.shape[1:], right.dtype)
+
+
+def halo_pass_on(copies):
+    for copy, _, _ in copies[:2]:
+        copy.wait_recv()
+    for copy, sends, _ in copies[4:]:
+        run_if(sends, copy.start)
 
 
 def halo_wait(copies):
-    for copy, sends, comes in copies:
+    for k, (copy, sends, comes) in enumerate(copies):
         run_if(sends, copy.wait_send)
-        run_if(comes, copy.wait_recv)
+        if k >= 2:
+            run_if(comes, copy.wait_recv)
 
 
 def halo_shapes(block):
     batch, rows, cols, channels = block.shape
     across = jax.ShapeDtypeStruct((batch, WIDTH, cols, channels), block.dtype)
-    along = jax.ShapeDtypeStruct((rows + 2 * WIDTH, batch * WIDTH, channels), block.dtype)
+    along = jax.ShapeDtypeStruct((3, batch * rows * WIDTH, channels), block.dtype)
     return (across, across, along, along)
 
 
 def pack_edges(block):
     batch, rows, cols, channels = block.shape
     sides = jnp.stack([block[:, :, :WIDTH], block[:, :, cols - WIDTH :]])
-    return sides.transpose(0, 2, 1, 3, 4).reshape(2, rows, batch * WIDTH, channels)
+    return sides.reshape(2, batch * rows * WIDTH, channels)
 
 
 def join_halo(block, low, high, left, right):
     batch, rows, cols, channels = block.shape
 
     def columns(side):
-        return side.reshape(rows + 2 * WIDTH, batch, WIDTH, channels).transpose(1, 0, 2, 3)
+        side = side.reshape(3, batch, rows, WIDTH, channels)
+        return jnp.concatenate([side[0, :, rows - WIDTH :], side[1], side[2, :, :WIDTH]], axis=1)
 
     middle = jnp.concatenate([low, block, high], axis=1)
     return jnp.concatenate([columns(left), middle, columns(right)], axis=2)
@@ -127,7 +128,7 @@
     lats, lons = lax.axis_size("lat"), lax.axis_size("lon")
     lat, lon = lax.axis_index("lat"), lax.axis_index("lon")
     peers = [lax.rem(lat + d, lats) for d in range(lats)]
-    friends = halo_friends(lat, lon, lats, lons)[:6] + [{"lat": p, "lon": lon} for p in peers[1:]]
+    friends = halo_friends(lat, lon, lats, lons)[:2] + [{"lat": p, "lon": lon} for p in peers[1:]]
     barrier = pltpu.get_barrier_semaphore()
     for friend in friends:
         pl.semaphore_signal(barrier, inc=1, device_id=friend, device_id_type=MESH)
@@ -142,6 +143,7 @@
         )
         for d in range(1, lats)
     ]
+    halo_pass_on(halo)
     halo_wait(halo)
     mine.wait()
     for copy in copies:
@@ -271,6 +273,7 @@
             start_remote(z_send.at[z_peers[d]], z_in.at[z], z_ssem.at[0, d], z_rsem.at[0, d], z_devices[d])
         )
     z_in[z] = z_send[z]
+    halo_pass_on(halo)
     for copy in copies:
         copy.wait()
     total = z_in[0]

time: 117 us -> 115 us (0.983)
  Pallas kernels: 92.6 us -> 89.5 us
    pallas_call x1, Pallas kernels: 37 us -> 32.3 us  [front_exchange(): pl.pallas_call(front_kernel, out_shape=halo_shapes(block) + (jax.ShapeDty...]
    reshape x8 -> x4, local copies, waits for them, and re-layouts: 3.03 us -> 0.9 us  [columns(): side = side.reshape(3, batch, rows, WIDTH, channels)]
    slice x0 -> x6, local copies, waits for them, and re-layouts: none -> 1.65 us  [the longest x2 0.89 us: pack_edges(): sides = jnp.stack([block[:, :, :WIDTH], block[:, :, cols - WIDTH:]])]
    pallas_call x1, Pallas kernels: 55.6 us -> 57.2 us  [sum_gradients(): pl.pallas_call(sum_kernel, out_shape=(jax.ShapeDtypeStruct(shape, bf16),...]
    another operation x0 -> x2, other arithmetic: none -> 1.23 us  [pack_edges(): sides = jnp.stack([block[:, :, :WIDTH], block[:, :, cols - WIDTH:]])]
    unnamed x45 -> x47, local copies, waits for them, and re-layouts: 5.35 us -> 6.06 us
where the time goes in v3:
time: 115 us; the launch traced here: 114 us
  Pallas kernels  89.5 us (78%)
  local copies, waits for them, and re-layouts  12.6 us (11%)
  other arithmetic  8.95 us (8%)
  matrix products  2.04 us (2%)
    pallas_call x1, Pallas kernels, sum_gradients(): pl.pallas_call(sum_kernel, out_shape=(jax.ShapeDtypeStruct(shape, bf16),...  57.2 us
    pallas_call x1, Pallas kernels, front_exchange(): pl.pallas_call(front_kernel, out_shape=halo_shapes(block) + (jax.ShapeDty...  32.3 us
    unnamed x47, local copies, waits for them, and re-layouts  6.06 us
    convert_element_type x1, other arithmetic, local(): (misfit.reshape(student.shape) + back_conv).astype(jnp.bfloat16)  2.49 us

profile of v3, /device:TPU:1, one launch (start us, length us, event | category | flops | bytes accessed | tf_op | source)
XLA Modules:
  0.0 114.1 jit_solution(17212174940513886406)
XLA Ops:
  0.6 0.0 copy-start
  0.7 0.9 fusion.111
  1.6 0.6 pad_maximum_fusion.edges
  2.2 0.1 copy.24
  2.3 0.7 reshape.160.sent
  3.0 32.3 %shard_map.102 = (bf16[2,3,32,256]{3,2,1,0:T(8,128)(2,1)}, bf16[2,3,32,256]{3,2,1,0:T(8,128)(2,1)}, bf16[3,24,256]{2,1,0:T(8,128)(2,1)}, bf16[3,24,256]{2,1,0:T(8,128)(2,1)}, bf16[16,16,256]{2,1,0:T(8,128)(2,1)}) custom-call(bf16[2,4,32,256]{3,2,1,0:T(8,128)(2,1)} %block.1, bf16[2,24,256]{2,1,0:T(8,128)(2,1)} %pad_maximum_fusion.edges, ...), custom_call_target="tpu_custom_call" | custom-call | tf_op jit(solution)/shard_map/pallas_call | solution.py:156
  35.3 1.0 reshape.171
  36.4 0.2 reshape.170
  36.6 0.6 copy-done.18
  37.2 0.0 copy-start.5
  37.3 0.7 copy-done.15
  38.1 0.1 copy-done.5
  38.1 0.1 copy-done.14
  38.2 0.1 maximum_convert_fusion
  38.3 0.7 copy-done.20
  39.1 1.8 %fusion.109 = (f32[2,4,32]{2,1,0:T(4,128)S(1)}, f32[2,4,32,256]{3,2,1,0:T(8,128)S(1)}) fusion(f32[2,10,38,256]{3,2,1,0:T(8,128)S(1)} %maximum_convert_fusion, f32[256]{0:T(256)S(1)} %bitcast.230, f32[256]{0:T(256)S(1)} %bitcast.232, f32[256]{0:T(256)S(1)} %bitcast.236, f32[256]{0:T(256)S(1)} %bitcast.238, f32[256]{0:T(256)S(1)} %bitcast.240, ...), kind=kLoop, calls=%fused_computation.243 | loop fusion | flops 6422272 | bytes 13158400 | tf_op jit(solution)/shard_map/reduce_sum | solution.py:427
  40.9 0.2 multiply_reduce_fusion.1
  41.1 0.1 rsqrt.12
  41.2 0.1 div.35
  41.3 0.6 copy-done.21
  41.9 0.1 multiply_convert_fusion.3.left_a
  42.1 0.0 copy-start.9
  42.1 0.0 copy-start.6
  42.1 0.5 multiply_convert_fusion
  42.6 0.1 copy-done.9
  42.7 0.4 copy-done.6
  43.2 0.3 copy-done.22
  43.4 0.3 multiply_convert_fusion.2
  43.8 0.8 fusion.right_a
  44.6 0.5 fusion.108
  45.0 0.3 copy-done.4
  45.4 0.6 fusion.56
  46.0 0.4 fusion.20
  46.4 0.5 fusion.38
  47.0 0.2 stack.220
  47.1 0.6 bitcast_bitcast_fusion.dw_ref
  47.8 0.6 pad_maximum_fusion.1.edges
  48.4 57.2 %shard_map.103 = (bf16[256,1024]{1,0:T(8,128)(2,1)}, bf16[256,1024]{1,0:T(8,128)(2,1)}, f32[2,64,128]{2,1,0:T(8,128)}, bf16[2,3,32,256]{3,2,1,0:T(8,128)(2,1)}, ...) custom-call(bf16[256,256]{1,0:T(8,128)(2,1)} %copy-done.9, ...), custom_call_target="tpu_custom_call" | custom-call | tf_op jit(solution)/shard_map/pallas_call | solution.py:344
  105.7 0.8 reshape.168
  106.5 0.7 slice.706
  107.4 0.1 copy-done.2
  107.5 0.7 copy-done.12
  108.2 0.1 maximum_convert_fusion.1
  108.3 2.5 %fusion.59 = bf16[2,4,32,256]{3,2,1,0:T(8,128)(2,1)} fusion(f32[2,4,32,256]{3,2,1,0:T(8,128)S(1)} %bitcast.208, f32[2,10,38,256]{3,2,1,0:T(8,128)S(1)} %maximum_convert_fusion.1, f32[256]{0:T(256)S(1)} %bitcast.231, f32[256]{0:T(256)S(1)} %bitcast.233, f32[256]{0:T(256)S(1)} %bitcast.237, f32[256]{0:T(256)S(1)} %bitcast.239, f32[256]{0:T(256)S(1)} %bitcast.241, ...), kind=kLoop, calls=%fused_computation.119 | loop fusion | flops 6488064 | bytes 13288448 | tf_op jit(solution)/shard_map/convert_element_type | solution.py:472
  110.8 1.1 convert_multiply_fusion.49
  111.9 0.1 multiply_bitcast_fusion
  112.1 1.3 %copy.18 = f32[1024,256]{1,0:T(8,128)} copy(f32[1024,256]{0,1:T(8,128)S(1)} %multiply_bitcast_fusion) | data formatting | bytes 2097152
  113.4 0.7 div.45
  (58 shorter events, 0.5 us)
Async XLA Ops:
  0.6 41.4 %copy-start = (bf16[256,1024]{1,0:T(8,128)(2,1)S(1)}, bf16[256,1024]{1,0:T(8,128)(2,1)}, u32[]{:S(2)}) copy-start(bf16[256,1024]{1,0:T(8,128)(2,1)} %param.11) | copy-start | bytes 1572868
  0.6 1.6 %copy-start.11 = (bf16[2,64,2,256]{3,2,1,0:T(2,128)(2,1)S(1)}, bf16[2,64,2,256]{3,2,1,0:T(2,128)(2,1)}, u32[]{:S(2)}) copy-start(bf16[2,64,2,256]{3,2,1,0:T(2,128)(2,1)} %param.8) | copy-start | bytes 393220
  36.4 0.8 copy-start.18
  36.4 0.8 copy-start.17
  37.2 0.9 copy-start.15
  37.2 0.9 copy-start.5
  37.2 0.9 copy-start.14
  38.2 0.8 copy-start.20
  41.2 0.7 copy-start.21
  42.1 0.7 copy-start.9
  42.1 1.1 copy-start.6
  42.7 1.0 copy-start.3
  42.7 0.7 copy-start.22
  43.8 0.8 copy-start.10
  44.6 0.8 copy-start.4
  46.0 1.7 %copy-start.1 = (bf16[256,256]{1,0:T(8,128)(2,1)}, bf16[256,256]{1,0:T(8,128)(2,1)S(1)}, u32[]{:S(2)}) copy-start(bf16[256,256]{1,0:T(8,128)(2,1)S(1)} %get-tuple-element.87) | copy-start | bytes 393220
  105.7 1.7 %copy-start.13 = (bf16[2,3,32,256]{3,2,1,0:T(8,128)(2,1)S(1)}, bf16[2,3,32,256]{3,2,1,0:T(8,128)(2,1)}, u32[]{:S(2)}) copy-start(bf16[2,3,32,256]{3,2,1,0:T(8,128)(2,1)} %get-tuple-element.23) | copy-start | bytes 294916
  106.5 0.8 copy-start.16
  106.5 0.9 copy-start.2
  107.3 0.9 copy-start.12
  108.3 2.5 %copy-start.8 = (bf16[256,1024]{1,0:T(8,128)(2,1)S(1)}, bf16[256,1024]{1,0:T(8,128)(2,1)}, u32[]{:S(2)}) copy-start(bf16[256,1024]{1,0:T(8,128)(2,1)} %get-tuple-element.25) | copy-start | bytes 1572868
  110.8 1.1 copy-start.7
  112.0 1.3 %copy-start.19 = (f32[2,64,128]{2,1,0:T(8,128)S(1)}, f32[2,64,128]{2,1,0:T(8,128)}, u32[]{:S(2)}) copy-start(f32[2,64,128]{2,1,0:T(8,128)} %get-tuple-element.27) | copy-start | bytes 196612

commit v4 on v3

v4 whole, which is shorter than its diff:
```python
import jax
import jax.numpy as jnp
from jax import lax
from jax.experimental import pallas as pl
from jax.experimental.pallas import tpu as pltpu
from jax.sharding import PartitionSpec as P

slope_coef = 0.7978845608028654
cubic_coef = 0.044715
norm_eps = 1e-06
MESH = pl.DeviceIdType.MESH

def start_remote(source, target, ssem, rsem, device_to):
    copy = pltpu.make_async_remote_copy(
        src_ref=source, dst_ref=target, send_sem=ssem, recv_sem=rsem,
        device_id=device_to, device_id_type=MESH,
    )
    copy.start()
    return copy


WIDTH = 3


def halo_friends(lat, lon, lats, lons):
    steps = [(0, 1), (0, -1), (1, 0), (-1, 0)]
    return [
        {"lat": lax.rem(lat + dl + lats, lats), "lon": lax.rem(lon + dn + lons, lons)}
        for dl, dn in steps
    ]


def halo_copies(block, edges, low, high, left, right, ssem, rsem):
    lats, lons = lax.axis_size("lat"), lax.axis_size("lon")
    lat, lon = lax.axis_index("lat"), lax.axis_index("lon")
    rows = block.shape[1]
    up = {"lat": jnp.minimum(lat + 1, lats - 1), "lon": lon}
    down = {"lat": jnp.maximum(lat - 1, 0), "lon": lon}
    first = lat == 0
    last = lat == lats - 1
    inner_up, inner_down = jnp.logical_not(last), jnp.logical_not(first)
    plan = [
        (edges.at[1], left.at[1], {"lat": lat, "lon": lax.rem(lon + 1, lons)}, None, None),
        (edges.at[0], right.at[1], {"lat": lat, "lon": lax.rem(lon + lons - 1, lons)}, None, None),
        (block.at[:, pl.ds(rows - WIDTH, WIDTH)], low, up, inner_up, inner_down),
        (block.at[:, pl.ds(0, WIDTH)], high, down, inner_down, inner_up),
        (left.at[1], left.at[0], up, inner_up, inner_down),
        (right.at[1], right.at[0], up, inner_up, inner_down),
        (left.at[1], left.at[2], down, inner_down, inner_up),
        (right.at[1], right.at[2], down, inner_down, inner_up),
    ]
    copies = []
    for k, (source, target, device_to, sends, comes) in enumerate(plan):
        copy = pltpu.make_async_remote_copy(
            src_ref=source, dst_ref=target, send_sem=ssem.at[k], recv_sem=rsem.at[k],
            device_id=device_to, device_id_type=MESH,
        )
        copies.append((copy, sends, comes))
    return copies


def run_if(condition, action):
    if condition is None:
        action()
    else:
        pl.when(condition)(action)


def halo_start(copies, low, high, left, right):
    lats, lat = lax.axis_size("lat"), lax.axis_index("lat")
    for copy, sends, _ in copies[:4]:
        run_if(sends, copy.start)

    @pl.when(lat == 0)
    def _():
        low[...] = jnp.zeros_like(low)
        left[0] = jnp.zeros(left.shape[1:], left.dtype)
        right[0] = jnp.zeros(right.shape[1:], right.dtype)

    @pl.when(lat == lats - 1)
    def _():
        high[...] = jnp.zeros_like(high)
        left[2] = jnp.zeros(left.shape[1:], left.dtype)
        right[2] = jnp.zeros(right.shape[1:], right.dtype)


def halo_pass_on(copies):
    for copy, _, _ in copies[:2]:
        copy.wait_recv()
    for copy, sends, _ in copies[4:]:
        run_if(sends, copy.start)


def halo_wait(copies):
    for k, (copy, sends, comes) in enumerate(copies):
        run_if(sends, copy.wait_send)
        if k >= 2:
            run_if(comes, copy.wait_recv)


def pack_edges(block, rows_f32, edges):
    batch, rows, cols, channels = block.shape
    for b in range(batch):
        for row in range(rows):
            at = (b * rows + row) * WIDTH
            line = block[b, row].astype(jnp.float32)
            rows_f32[0, at : at + WIDTH] = line[:WIDTH]
            rows_f32[1, at : at + WIDTH] = line[cols - WIDTH :]
    edges[...] = rows_f32[...].astype(edges.dtype)


def fill_padded(padded, edge_rows, block, low, high, left, right):
    batch, rows, cols, channels = block.shape
    for side, ref in enumerate((left, right)):
        for k in range(3):
            edge_rows[side, k] = ref[k].astype(jnp.float32)
    for b in range(batch):
        for row in range(rows + 2 * WIDTH):
            if row < WIDTH:
                line, k, r = low[b, row], 0, rows - WIDTH + row
            elif row < WIDTH + rows:
                line, k, r = block[b, row - WIDTH], 1, row - WIDTH
            else:
                line, k, r = high[b, row - WIDTH - rows], 2, row - WIDTH - rows
            at = (b * rows + r) * WIDTH
            padded[b, row, WIDTH : WIDTH + cols] = line.astype(jnp.float32)
            padded[b, row, :WIDTH] = edge_rows[0, k, at : at + WIDTH]
            padded[b, row, WIDTH + cols : 2 * WIDTH + cols] = edge_rows[1, k, at : at + WIDTH]


def run_stencil(padded, weight, shape, flipped, emit):
    batch, rows, cols, channels = shape
    size = weight.shape[0]

    @pl.loop(0, batch * rows)
    def _(n):
        b, row = n // rows, lax.rem(n, rows)
        total = jnp.zeros((cols, channels), jnp.float32)
        for p in range(size):
            for q in range(size):
                row_at = size - 1 - p if flipped else p
                col_at = size - 1 - q if flipped else q
                total = total + weight[p, q : q + 1] * padded[b, row + row_at, col_at : col_at + cols]
        emit(n, b, row, total)


def tap_sums(padded, cell_grad, shape, size, dw):
    batch, rows, cols, channels = shape
    dw[...] = jnp.zeros_like(dw)

    @pl.loop(0, size)
    def _(p):
        for q in range(size):
            total = jnp.zeros((TILE, channels), jnp.float32)
            for n in range(batch * rows):
                b, row = n // rows, n % rows
                product = padded[b, row + p, q : q + cols] * cell_grad[n * cols : (n + 1) * cols]
                for t in range(cols // TILE):
                    total = total + product[t * TILE : (t + 1) * TILE]
            line = jnp.sum(total, axis=0, keepdims=True)
            for half in range(2):
                dw[half, pl.ds(p * TILE + q, 1)] = line[:, half * SIDE : (half + 1) * SIDE]


BLOCKS, SIDE, SPLIT, TILE, DW_ROWS, DW_PAD = 16, 128, 64, 8, 4, 16
LOWER = SIDE - SPLIT + DW_PAD
CHIPS_Z = 16
CHUNK = 256


def step_kernel(
    block, sent, weight, gain, w_in, w_out, scale,
    out_a, out_b, out_dw, out_grad_ref,
    edge_f32, edges, low, high, left, right, edge_rows, padded, came, came_f32, target,
    smoothed, unit, hid, slope, misfit, cell_grad, grad_block,
    edges2, low2h, high2h, left2h, right2h, padded2, dw_ref,
    own, other, dw_other, top, low_part, top_in1, low_in1, top1, low1, top_in2, low_in2,
    z_send, z_in, z_own, z_all, top_g1, low_g1, top_all, low_all,
    core_ssem, core_rsem, xy_ssem, xy_rsem, z_ssem, z_rsem, halo_ssem, halo_rsem,
    halo2_ssem, halo2_rsem, teach_ssem, teach_rsem, local_sem,
):
    f32, bf16 = jnp.float32, jnp.bfloat16
    lats, lons = lax.axis_size("lat"), lax.axis_size("lon")
    lat, lon = lax.axis_index("lat"), lax.axis_index("lon")
    core = lax.rem(lat, 2)
    z = lax.rem(lon, 2) * 8 + lat // 2
    x = lon // 8
    y = lax.rem(lon // 2, 4)

    def device(core_to, z_to, x_to, y_to):
        return {
            "lat": lax.rem(z_to, 8) * 2 + core_to,
            "lon": x_to * 8 + y_to * 2 + z_to // 8,
        }

    partner = device(1 - core, z, x, y)
    x_peers = [lax.rem(x + d, 4) for d in range(4)]
    y_peers = [lax.rem(y + d, 4) for d in range(4)]
    z_peers = [lax.rem(z + d, CHIPS_Z) for d in range(CHIPS_Z)]
    x_devices = [device(core, z, p, y) for p in x_peers]
    y_devices = [device(core, z, x, p) for p in y_peers]
    z_devices = [device(core, p, x, y) for p in z_peers]

    barrier = pltpu.get_barrier_semaphore()
    friends = [partner] + x_devices[1:] + y_devices[1:] + z_devices[1:]
    lat_peers = [lax.rem(lat + d, lats) for d in range(lats)]
    friends = friends + halo_friends(lat, lon, lats, lons)[:2]
    friends = friends + [{"lat": p, "lon": lon} for p in lat_peers[1:]]
    for friend in friends:
        pl.semaphore_signal(barrier, inc=1, device_id=friend, device_id_type=MESH)

    mine = pltpu.make_async_copy(sent.at[lat], came.at[lat], local_sem)
    mine.start()
    pack_edges(block, edge_f32, edges)
    pl.semaphore_wait(barrier, len(friends))

    front = halo_copies(block, edges, low, high, left, right, halo_ssem, halo_rsem)
    halo_start(front, low, high, left, right)
    teaching = [
        start_remote(
            sent.at[lat_peers[d]], came.at[lat], teach_ssem.at[d], teach_rsem.at[d],
            {"lat": lat_peers[d], "lon": lon},
        )
        for d in range(1, lats)
    ]
    halo_pass_on(front)
    halo_wait(front)
    fill_padded(padded, edge_rows, block, low, high, left, right)

    shape = block.shape
    batch, rows, cols, channels = shape

    def keep(n, b, row, total):
        smoothed[pl.ds(pl.multiple_of(n * cols, cols), cols)] = total

    run_stencil(padded, weight, shape, False, keep)
    smooth = smoothed[...]
    average = jnp.mean(smooth, axis=-1, keepdims=True)
    centred = smooth - average
    variance = jnp.mean(centred * centred, axis=-1, keepdims=True)
    inv_std = lax.rsqrt(variance + norm_eps)
    unit[...] = centred * inv_std
    normed = (unit[...] * gain[...]).astype(bf16)
    mlp_out = jnp.zeros((batch * rows * cols, channels), f32)
    hidden_size = w_in.shape[1]
    for at in range(0, hidden_size, CHUNK):
        preact = jnp.dot(normed, w_in[:, at : at + CHUNK], preferred_element_type=f32)
        tangent = jnp.tanh(slope_coef * (preact + cubic_coef * preact * preact * preact))
        hidden = (0.5 * preact * (1.0 + tangent)).astype(bf16)
        hid[:, at : at + CHUNK] = hidden
        slope[:, at : at + CHUNK] = 0.5 * (1.0 + tangent) + 0.5 * preact * (
            1.0 - tangent * tangent
        ) * slope_coef * (1.0 + 3.0 * cubic_coef * preact * preact)
        mlp_out = mlp_out + jnp.dot(hidden, w_out[at : at + CHUNK], preferred_element_type=f32)

    mine.wait()
    for copy in teaching:
        copy.wait()
    for src in range(lats):
        came_f32[src] = came[src].astype(f32)
    part = cols // lats
    for src in range(lats):
        for n in range(batch * rows):
            at = n * cols + src * part
            target[at : at + part] = came_f32[src, n * part : (n + 1) * part]
    student = jnp.concatenate(
        [block[n // rows, n % rows] for n in range(batch * rows)], axis=0
    ).astype(f32)
    misfit[...] = (student + scale[...] * mlp_out) - target[...]
    out_grad = (scale[...] * misfit[...]).astype(bf16)
    contract_cells = (((0,), (0,)), ((), ()))
    contract_last = (((1,), (1,)), ((), ()))

    def keep_product(which, at, product):
        for row in range(channels // SIDE):
            for col in range(CHUNK // SIDE):
                own[which, row * 8 + at // SIDE + col] = product[
                    row * SIDE : (row + 1) * SIDE, col * SIDE : (col + 1) * SIDE
                ]

    normed_grad = jnp.zeros((batch * rows * cols, channels), f32)
    for at in range(0, hidden_size, CHUNK):
        hidden_grad = lax.dot_general(
            out_grad, w_out[at : at + CHUNK], contract_last, preferred_element_type=f32
        )
        preact_grad = (hidden_grad * slope[:, at : at + CHUNK]).astype(bf16)
        keep_product(
            0, at, lax.dot_general(normed, preact_grad, contract_cells, preferred_element_type=f32)
        )
        keep_product(
            1,
            at,
            lax.dot_general(
                out_grad, hid[:, at : at + CHUNK], contract_cells, preferred_element_type=f32
            ),
        )
        normed_grad = normed_grad + lax.dot_general(
            preact_grad, w_in[:, at : at + CHUNK], contract_last, preferred_element_type=f32
        )
    core_copies = [
        start_remote(own.at[1 - core], other, core_ssem.at[0], core_rsem.at[0], partner)
    ]
    unit_grad = normed_grad * gain[...]
    unit_norm = unit[...]
    first_mean = jnp.mean(unit_grad, axis=-1, keepdims=True)
    second_mean = jnp.mean(unit_grad * unit_norm, axis=-1, keepdims=True)
    conv_grad = (inv_std * (unit_grad - first_mean - unit_norm * second_mean)).astype(bf16)
    for n in range(batch * rows):
        grad_block[n // rows, n % rows] = conv_grad[n * cols : (n + 1) * cols]
    cell_grad[...] = conv_grad.astype(f32)
    pack_edges(grad_block, edge_f32, edges2)
    halo = halo_copies(
        grad_block, edges2, low2h, high2h, left2h, right2h, halo2_ssem, halo2_rsem
    )
    halo_start(halo, low2h, high2h, left2h, right2h)
    tap_sums(padded, cell_grad, shape, weight.shape[0], dw_ref)
    copies = core_copies + [
        start_remote(dw_ref.at[1 - core], dw_other, core_ssem.at[1], core_rsem.at[1], partner),
    ]
    for copy in copies:
        copy.wait()
    for block in range(BLOCKS):
        bx, by = block // 4, block % 4
        top[bx, by] = own[core, block, :SPLIT] + other[block, :SPLIT]
        low_part[by, bx, : SIDE - SPLIT] = own[core, block, SPLIT:] + other[block, SPLIT:]
        rows = slice(DW_ROWS * block, DW_ROWS * (block + 1))
        dw_sum = dw_ref[core, rows] + dw_other[rows]
        low_part[by, bx, SIDE - SPLIT :] = jnp.concatenate(
            [dw_sum, jnp.zeros((DW_PAD - DW_ROWS, SIDE), jnp.float32)], axis=0
        )

    copies = []
    for d in (2, 1, 3):
        copies.append(
            start_remote(top.at[x_peers[d]], top_in1.at[d], xy_ssem.at[0, d], xy_rsem.at[0, d], x_devices[d])
        )
        copies.append(
            start_remote(low_part.at[y_peers[d]], low_in1.at[d], xy_ssem.at[1, d], xy_rsem.at[1, d], y_devices[d])
        )
    for copy in copies:
        copy.wait()
    top1[...] = top[x] + top_in1[1] + top_in1[2] + top_in1[3]
    low1[...] = low_part[y] + low_in1[1] + low_in1[2] + low_in1[3]

    copies = []
    for d in (2, 1, 3):
        copies.append(
            start_remote(top1.at[y_peers[d]], top_in2.at[d], xy_ssem.at[2, d], xy_rsem.at[2, d], y_devices[d])
        )
        copies.append(
            start_remote(low1.at[x_peers[d]], low_in2.at[d], xy_ssem.at[3, d], xy_rsem.at[3, d], x_devices[d])
        )
    for copy in copies:
        copy.wait()
    top2 = top1[y] + top_in2[1] + top_in2[2] + top_in2[3]
    low2 = low1[x] + low_in2[1] + low_in2[2] + low_in2[3]
    for tile in range(CHIPS_Z):
        at = TILE * tile
        z_send[tile, :TILE] = top2[at : at + TILE] if at < SPLIT else low2[at - SPLIT : at - SPLIT + TILE]
        z_send[tile, TILE:] = low2[SIDE - SPLIT : SIDE - SPLIT + TILE]

    order = [8, 7, 9, 6, 10, 5, 11, 4, 12, 3, 13, 2, 14, 1, 15]
    copies = []
    for d in order:
        copies.append(
            start_remote(z_send.at[z_peers[d]], z_in.at[z], z_ssem.at[0, d], z_rsem.at[0, d], z_devices[d])
        )
    z_in[z] = z_send[z]
    halo_pass_on(halo)
    for copy in copies:
        copy.wait()
    total = z_in[0]
    for tile in range(1, CHIPS_Z):
        total = total + z_in[tile]
    z_own[...] = total

    copies = []
    for d in order:
        copies.append(
            start_remote(z_own.at[:TILE], z_all.at[z], z_ssem.at[1, d], z_rsem.at[1, d], z_devices[d])
        )
    z_all[z] = z_own[:TILE]
    for copy in copies:
        copy.wait()
    tiles = z_all[...].reshape(SIDE, SIDE)
    dw_tile = jnp.concatenate(
        [z_own[TILE:], jnp.zeros((DW_PAD - TILE, SIDE), jnp.float32)], axis=0
    )
    top_g1[y] = tiles[:SPLIT].astype(jnp.bfloat16)
    low_g1[x] = jnp.concatenate([tiles[SPLIT:], dw_tile], axis=0).astype(jnp.bfloat16)

    copies = []
    for d in (2, 1, 3):
        copies.append(
            start_remote(top_g1.at[y], top_g1.at[y], xy_ssem.at[4, d], xy_rsem.at[4, d], y_devices[d])
        )
        copies.append(
            start_remote(low_g1.at[x], low_g1.at[x], xy_ssem.at[5, d], xy_rsem.at[5, d], x_devices[d])
        )
    for copy in copies:
        copy.wait()

    copies = []
    for d in (2, 1, 3):
        copies.append(
            start_remote(top_g1, top_all.at[core, x], xy_ssem.at[6, d], xy_rsem.at[6, d], x_devices[d])
        )
        copies.append(
            start_remote(low_g1, low_all.at[core, y], xy_ssem.at[7, d], xy_rsem.at[7, d], y_devices[d])
        )
    top_all[core, x] = top_g1[...]
    low_all[core, y] = low_g1[...]
    halo_wait(halo)
    fill_padded(padded2, edge_rows, grad_block, low2h, high2h, left2h, right2h)

    def finish(n, b, row, total):
        cells = pl.ds(pl.multiple_of(n * cols, cols), cols)
        out_grad_ref[b, row] = (misfit[cells] + total).astype(bf16)

    run_stencil(padded2, weight, shape, True, finish)
    for copy in copies:
        copy.wait()

    copies = [
        start_remote(top_all.at[core], top_all.at[core], core_ssem.at[2], core_rsem.at[2], partner),
        start_remote(low_all.at[core], low_all.at[core], core_ssem.at[3], core_rsem.at[3], partner),
    ]
    for copy in copies:
        copy.wait()
    for which, out in enumerate((out_a, out_b)):
        for block in range(BLOCKS):
            bx, by = block // 4, block % 4
            row, col = SIDE * (block // 8), SIDE * (block % 8)
            out[row : row + SPLIT, col : col + SIDE] = top_all[which, bx, by]
            out[row + SPLIT : row + SIDE, col : col + SIDE] = low_all[which, by, bx, : SIDE - SPLIT]
            dw_rows = low_all[which, by, bx, SIDE - SPLIT :].astype(jnp.float32)[:DW_ROWS]
            out_dw[which, DW_ROWS * block : DW_ROWS * (block + 1)] = dw_rows


def whole_step(block, sent, weight, gain, w_in, w_out, scale):
    f32, bf16 = jnp.float32, jnp.bfloat16
    batch, rows, cols, channels = block.shape
    cells, lats = batch * rows * cols, sent.shape[0]
    edge_cells = batch * rows * WIDTH
    vmem = pl.BlockSpec(memory_space=pltpu.VMEM)
    across = pltpu.VMEM((batch, WIDTH, cols, channels), bf16)
    along = pltpu.VMEM((3, edge_cells, channels), bf16)
    padded = pltpu.VMEM((batch, rows + 2 * WIDTH, cols + 2 * WIDTH + 2, channels), f32)
    dw_shape = (2, BLOCKS * DW_ROWS, SIDE)
    cell_f32 = pltpu.VMEM((cells, channels), f32)
    return pl.pallas_call(
        step_kernel,
        out_shape=(
            jax.ShapeDtypeStruct(w_in.shape, bf16),
            jax.ShapeDtypeStruct(w_in.shape, bf16),
            jax.ShapeDtypeStruct(dw_shape, f32),
            jax.ShapeDtypeStruct(block.shape, bf16),
        ),
        in_specs=[vmem] * 7,
        out_specs=(vmem,) * 4,
        scratch_shapes=[
            pltpu.VMEM((2, edge_cells, channels), f32),
            pltpu.VMEM((2, edge_cells, channels), bf16),
            across,
            across,
            along,
            along,
            pltpu.VMEM((2, 3, edge_cells, channels), f32),
            padded,
            pltpu.VMEM(sent.shape, bf16),
            pltpu.VMEM(sent.shape, f32),
            cell_f32,
            cell_f32,
            cell_f32,
            pltpu.VMEM((cells, w_in.shape[1]), bf16),
            pltpu.VMEM((cells, w_in.shape[1]), f32),
            cell_f32,
            cell_f32,
            pltpu.VMEM(block.shape, bf16),
            pltpu.VMEM((2, edge_cells, channels), bf16),
            across,
            across,
            along,
            along,
            padded,
            pltpu.VMEM(dw_shape, f32),
            pltpu.VMEM((2, BLOCKS, SIDE, SIDE), f32),
            pltpu.VMEM((BLOCKS, SIDE, SIDE), f32),
            pltpu.VMEM(dw_shape[1:], f32),
            pltpu.VMEM((4, 4, SPLIT, SIDE), f32),
            pltpu.VMEM((4, 4, LOWER, SIDE), f32),
            pltpu.VMEM((4, 4, SPLIT, SIDE), f32),
            pltpu.VMEM((4, 4, LOWER, SIDE), f32),
            pltpu.VMEM((4, SPLIT, SIDE), f32),
            pltpu.VMEM((4, LOWER, SIDE), f32),
            pltpu.VMEM((4, SPLIT, SIDE), f32),
            pltpu.VMEM((4, LOWER, SIDE), f32),
            pltpu.VMEM((CHIPS_Z, 2 * TILE, SIDE), f32),
            pltpu.VMEM((CHIPS_Z, 2 * TILE, SIDE), f32),
            pltpu.VMEM((2 * TILE, SIDE), f32),
            pltpu.VMEM((CHIPS_Z, TILE, SIDE), f32),
            pltpu.VMEM((4, SPLIT, SIDE), bf16),
            pltpu.VMEM((4, LOWER, SIDE), bf16),
            pltpu.VMEM((2, 4, 4, SPLIT, SIDE), bf16),
            pltpu.VMEM((2, 4, 4, LOWER, SIDE), bf16),
            pltpu.SemaphoreType.DMA((4,)),
            pltpu.SemaphoreType.DMA((4,)),
            pltpu.SemaphoreType.DMA((8, 4)),
            pltpu.SemaphoreType.DMA((8, 4)),
            pltpu.SemaphoreType.DMA((2, CHIPS_Z)),
            pltpu.SemaphoreType.DMA((2, CHIPS_Z)),
            pltpu.SemaphoreType.DMA((8,)),
            pltpu.SemaphoreType.DMA((8,)),
            pltpu.SemaphoreType.DMA((8,)),
            pltpu.SemaphoreType.DMA((8,)),
            pltpu.SemaphoreType.DMA((lats,)),
            pltpu.SemaphoreType.DMA((lats,)),
            pltpu.SemaphoreType.DMA,
        ],
        compiler_params=pltpu.CompilerParams(collective_id=0, has_side_effects=True),
    )(block, sent, weight, gain, w_in, w_out, scale)


def local(student, teacher, dw_weight, norm_gain, w_in, w_out, layer_scale):
    batch_size, tile_rows, tile_cols, channel_count = student.shape
    kernel_size = dw_weight.shape[0]
    lats = lax.axis_size("lat")
    cell_total = batch_size * tile_rows * lats * tile_cols * lax.axis_size("lon")
    sent = teacher.reshape(batch_size, lats, -1, teacher.shape[2], channel_count)
    sent = sent.transpose(1, 0, 2, 3, 4).reshape(lats, -1, channel_count)
    sum_in, sum_out, sum_dw, grad_student = whole_step(
        student, sent, dw_weight, norm_gain[None], w_in, w_out, layer_scale[None]
    )
    sum_dw = sum_dw[:, : kernel_size * TILE].reshape(2, kernel_size, TILE, SIDE)
    sum_dw = sum_dw[:, :, :kernel_size].transpose(1, 2, 0, 3)
    sum_dw = sum_dw.reshape(kernel_size, kernel_size, channel_count)
    return (
        grad_student,
        sum_in.astype(jnp.float32) / cell_total,
        sum_out.T.astype(jnp.float32) / cell_total,
        sum_dw / cell_total,
    )


def solution(mesh):
    placed = (
        P(None, "lat", "lon", None),
        P(None, None, ("lon", "lat"), None),
        P(),
        P(),
        P(),
        P(),
        P(),
    )
    return jax.shard_map(
        local,
        mesh=mesh,
        in_specs=placed,
        out_specs=(P(None, "lat", "lon", None), P(), P(), P()),
        check_vma=False,
    )
```

time: 115 us -> 92.4 us (0.80)
  local copies, waits for them, and re-layouts: 12.6 us -> 5.19 us
  other arithmetic: 8.95 us -> 2.45 us
  Pallas kernels: 89.5 us -> 83.9 us
  matrix products: 2.04 us -> 0 us
    pallas_call x2 -> x1, Pallas kernels: 89.5 us -> 83.9 us  [whole_step(): pl.pallas_call(step_kernel, out_shape=(jax.ShapeDtypeStruct(w_in.shape, b...]
    unnamed x47 -> x4, local copies, waits for them, and re-layouts: 6.06 us -> 1.96 us
    reduce_sum x5 -> x0, other arithmetic: 3.62 us -> none  [the longest x1 1.84 us: local(): average = jnp.mean(smoothed, axis=-1, keepdims=True)]
    convert_element_type x4 -> x0, other arithmetic: 2.88 us -> none  [the longest x1 2.49 us: local(): (misfit.reshape(student.shape) + back_conv).astype(jnp.bfloat16)]
    div x1, other arithmetic: 0.11 us -> 2.44 us  [local(): sum_out.T.astype(jnp.float32) / cell_total]
    dot_general x4 -> x0, matrix products: 2.04 us -> none  [the longest x1 0.78 us: local(): lax.dot_general(out_grad, w_out, (((1,), (1,)), ((), ())), preferred_elem...]
    slice x9 -> x0, local copies, waits for them, and re-layouts: 1.69 us -> none  [the longest x2 0.89 us: pack_edges(): sides = jnp.stack([block[:, :, :WIDTH], block[:, :, cols - WIDTH:]])]
    convert_element_type x3 -> x0, local copies, waits for them, and re-layouts: 1.26 us -> none  [local(): misfit = output - target.reshape(-1, channel_count).astype(jnp.float32)]
where the time goes in v4:
time: 92.4 us; the launch traced here: 92.2 us
  Pallas kernels  83.9 us (91%)
  local copies, waits for them, and re-layouts  5.19 us (6%)
  other arithmetic  2.45 us (3%)
    pallas_call x1, Pallas kernels, whole_step(): pl.pallas_call(step_kernel, out_shape=(jax.ShapeDtypeStruct(w_in.shape, b...  83.9 us
    div x1, other arithmetic, local(): sum_out.T.astype(jnp.float32) / cell_total  2.44 us
    unnamed x4, local copies, waits for them, and re-layouts  1.96 us

profile of v4, /device:TPU:1, one launch (start us, length us, event | category | flops | bytes accessed | tf_op | source)
XLA Modules:
  0.0 92.2 jit_solution(15003940372896062091)
XLA Ops:
  0.6 1.0 %copy.15 = bf16[2,16,4,2,256]{4,3,2,0,1:T(2,128)(2,1)S(1)} copy(bf16[2,16,4,2,256]{4,3,2,1,0:T(2,128)(2,1)} %bitcast.13) | data formatting | bytes 262144 | tf_op jit(solution)/shard_map/reshape | solution.py:529
  1.6 0.7 reshape.21.sent
  2.3 83.9 %shard_map.102 = (bf16[256,1024]{1,0:T(8,128)(2,1)}, bf16[256,1024]{1,0:T(8,128)(2,1)}, f32[2,64,128]{2,1,0:T(8,128)}, bf16[2,4,32,256]{3,2,1,0:T(8,128)(2,1)}) custom-call(bf16[2,4,32,256]{3,2,1,0:T(8,128)(2,1)} %block.1, bf16[16,16,256]{2,1,0:T(8,128)(2,1)} %reshape.21.sent, f32[7,7,256]{2,1,0:T(8,128)} %weight.1, f32[1,256]{1,0:T(1,128)} %bitcast.14, ...), custom_call_target="tpu_custom_call" | custom-call | tf_op jit(solution)/shard_map/pallas_call | solution.py:451
  86.3 0.8 slice_bitcast_fusion
  87.1 0.7 div.29
  87.8 2.4 %multiply_bitcast_fusion = (f32[1024,256]{0,1:T(8,128)S(1)}, f32[256,1024]{1,0:T(8,128)}) fusion(bf16[256,1024]{1,0:T(8,128)(2,1)} %get-tuple-element.10, bf16[256,1024]{1,0:T(8,128)(2,1)} %get-tuple-element.9), kind=kLoop, calls=%fused_computation | loop fusion | flops 1048576 | bytes 3145728 | tf_op jit(solution)/shard_map/div | solution.py:540
  90.2 0.0 copy-start
  90.2 1.3 %copy.13 = f32[1024,256]{1,0:T(8,128)} copy(f32[1024,256]{0,1:T(8,128)S(1)} %get-tuple-element.16) | data formatting | bytes 2097152
  91.6 0.0 copy-done
  91.6 0.7 copy.17
  (2 shorter events, 0.0 us)
Async XLA Ops:
  90.2 1.3 %copy-start = (bf16[2,4,32,256]{3,2,1,0:T(8,128)(2,1)S(1)}, bf16[2,4,32,256]{3,2,1,0:T(8,128)(2,1)}, u32[]{:S(2)}) copy-start(bf16[2,4,32,256]{3,2,1,0:T(8,128)(2,1)} %get-tuple-element.22) | copy-start | bytes 393220

commit v5 on v4

--- a/solution.py
+++ b/solution.py
@@ -168,16 +168,20 @@
 CHUNK = 256
 
 
+def block_slot(which, row, col):
+    return row * 8 + col if which == 0 else row * 2 + col
+
+
 def step_kernel(
     block, sent, weight, gain, w_in, w_out, scale,
     out_a, out_b, out_dw, out_grad_ref,
     edge_f32, edges, low, high, left, right, edge_rows, padded, came, came_f32, target,
     smoothed, unit, hid, slope, misfit, cell_grad, grad_block,
     edges2, low2h, high2h, left2h, right2h, padded2, dw_ref,
-    own, other, dw_other, top, low_part, top_in1, low_in1, top1, low1, top_in2, low_in2,
-    z_send, z_in, z_own, z_all, top_g1, low_g1, top_all, low_all,
+    own, other, dw_other, top, low_part, top_b, low_b, top_in1, low_in1, top1, low1, top_in2, low_in2,
+    z_send, z_in, z_own, z_all, dw_send, dw_in, dw_sum_ref, dw_done, top_g1, low_g1, top_all, low_all,
     core_ssem, core_rsem, xy_ssem, xy_rsem, z_ssem, z_rsem, halo_ssem, halo_rsem,
-    halo2_ssem, halo2_rsem, teach_ssem, teach_rsem, local_sem,
+    halo2_ssem, halo2_rsem, teach_ssem, teach_rsem, local_sem, dw_ssem, dw_rsem, pair_ssem, pair_rsem,
 ):
     f32, bf16 = jnp.float32, jnp.bfloat16
     lats, lons = lax.axis_size("lat"), lax.axis_size("lon")
@@ -271,10 +275,11 @@
     contract_cells = (((0,), (0,)), ((), ()))
     contract_last = (((1,), (1,)), ((), ()))
 
-    def keep_product(which, at, product):
-        for row in range(channels // SIDE):
-            for col in range(CHUNK // SIDE):
-                own[which, row * 8 + at // SIDE + col] = product[
+    def keep_product(which, row_at, col_at, product):
+        for row in range(product.shape[0] // SIDE):
+            for col in range(product.shape[1] // SIDE):
+                slot = block_slot(which, row_at // SIDE + row, col_at // SIDE + col)
+                own[which, slot] = product[
                     row * SIDE : (row + 1) * SIDE, col * SIDE : (col + 1) * SIDE
                 ]
 
@@ -285,13 +290,14 @@
         )
         preact_grad = (hidden_grad * slope[:, at : at + CHUNK]).astype(bf16)
         keep_product(
-            0, at, lax.dot_general(normed, preact_grad, contract_cells, preferred_element_type=f32)
+            0, 0, at, lax.dot_general(normed, preact_grad, contract_cells, preferred_element_type=f32)
         )
         keep_product(
             1,
             at,
+            0,
             lax.dot_general(
-                out_grad, hid[:, at : at + CHUNK], contract_cells, preferred_element_type=f32
+                hid[:, at : at + CHUNK], out_grad, contract_cells, preferred_element_type=f32
             ),
         )
         normed_grad = normed_grad + lax.dot_general(
@@ -329,18 +335,23 @@
             [dw_sum, jnp.zeros((DW_PAD - DW_ROWS, SIDE), jnp.float32)], axis=0
         )
 
+    for k in range(4):
+        top_b[k] = top[k].astype(bf16)
+        low_b[k] = low_part[k].astype(bf16)
     copies = []
     for d in (2, 1, 3):
         copies.append(
-            start_remote(top.at[x_peers[d]], top_in1.at[d], xy_ssem.at[0, d], xy_rsem.at[0, d], x_devices[d])
-        )
-        copies.append(
-            start_remote(low_part.at[y_peers[d]], low_in1.at[d], xy_ssem.at[1, d], xy_rsem.at[1, d], y_devices[d])
+            start_remote(top_b.at[x_peers[d]], top_in1.at[d], xy_ssem.at[0, d], xy_rsem.at[0, d], x_devices[d])
+        )
+        copies.append(
+            start_remote(low_b.at[y_peers[d]], low_in1.at[d], xy_ssem.at[1, d], xy_rsem.at[1, d], y_devices[d])
         )
     for copy in copies:
         copy.wait()
-    top1[...] = top[x] + top_in1[1] + top_in1[2] + top_in1[3]
-    low1[...] = low_part[y] + low_in1[1] + low_in1[2] + low_in1[3]
+    top1[...] = top[x] + top_in1[1].astype(f32) + top_in1[2].astype(f32) + top_in1[3].astype(f32)
+    low1[...] = (
+        low_part[y] + low_in1[1].astype(f32) + low_in1[2].astype(f32) + low_in1[3].astype(f32)
+    )
 
     copies = []
     for d in (2, 1, 3):
@@ -356,8 +367,8 @@
     low2 = low1[x] + low_in2[1] + low_in2[2] + low_in2[3]
     for tile in range(CHIPS_Z):
         at = TILE * tile
-        z_send[tile, :TILE] = top2[at : at + TILE] if at < SPLIT else low2[at - SPLIT : at - SPLIT + TILE]
-        z_send[tile, TILE:] = low2[SIDE - SPLIT : SIDE - SPLIT + TILE]
+        z_send[tile] = top2[at : at + TILE] if at < SPLIT else low2[at - SPLIT : at - SPLIT + TILE]
+    dw_send[...] = low2[SIDE - SPLIT : SIDE - SPLIT + TILE]
 
     order = [8, 7, 9, 6, 10, 5, 11, 4, 12, 3, 13, 2, 14, 1, 15]
     copies = []
@@ -365,6 +376,20 @@
         copies.append(
             start_remote(z_send.at[z_peers[d]], z_in.at[z], z_ssem.at[0, d], z_rsem.at[0, d], z_devices[d])
         )
+    owner = x * 4 + y
+    is_owner = z == owner
+    toward = lax.rem(owner - z + CHIPS_Z, CHIPS_Z)
+    away = lax.rem(z - owner + CHIPS_Z, CHIPS_Z)
+    dw_copy = pltpu.make_async_remote_copy(
+        src_ref=dw_send, dst_ref=dw_in.at[z], send_sem=dw_ssem.at[0], recv_sem=dw_rsem.at[0, toward],
+        device_id=device(core, owner, x, y), device_id_type=MESH,
+    )
+    pl.when(jnp.logical_not(is_owner))(dw_copy.start)
+
+    @pl.when(is_owner)
+    def _():
+        dw_in[z] = dw_send[...]
+
     z_in[z] = z_send[z]
     halo_pass_on(halo)
     for copy in copies:
@@ -374,42 +399,33 @@
         total = total + z_in[tile]
     z_own[...] = total
 
+    def dw_spread(d):
+        return pltpu.make_async_remote_copy(
+            src_ref=dw_sum_ref, dst_ref=dw_done, send_sem=dw_ssem.at[d], recv_sem=dw_rsem.at[1, d],
+            device_id=z_devices[d], device_id_type=MESH,
+        )
+
+    @pl.when(is_owner)
+    def _():
+        for d in range(1, CHIPS_Z):
+            pltpu.make_async_remote_copy(
+                src_ref=dw_send, dst_ref=dw_in.at[z], send_sem=dw_ssem.at[0],
+                recv_sem=dw_rsem.at[0, d], device_id=partner, device_id_type=MESH,
+            ).wait_recv()
+        dw_total = dw_in[0]
+        for tile in range(1, CHIPS_Z):
+            dw_total = dw_total + dw_in[tile]
+        dw_sum_ref[...] = dw_total
+        for d in order:
+            dw_spread(d).start()
+        dw_done[...] = dw_total
+
     copies = []
     for d in order:
         copies.append(
-            start_remote(z_own.at[:TILE], z_all.at[z], z_ssem.at[1, d], z_rsem.at[1, d], z_devices[d])
-        )
-    z_all[z] = z_own[:TILE]
-    for copy in copies:
-        copy.wait()
-    tiles = z_all[...].reshape(SIDE, SIDE)
-    dw_tile = jnp.concatenate(
-        [z_own[TILE:], jnp.zeros((DW_PAD - TILE, SIDE), jnp.float32)], axis=0
-    )
-    top_g1[y] = tiles[:SPLIT].astype(jnp.bfloat16)
-    low_g1[x] = jnp.concatenate([tiles[SPLIT:], dw_tile], axis=0).astype(jnp.bfloat16)
-
-    copies = []
-    for d in (2, 1, 3):
-        copies.append(
-            start_remote(top_g1.at[y], top_g1.at[y], xy_ssem.at[4, d], xy_rsem.at[4, d], y_devices[d])
-        )
-        copies.append(
-            start_remote(low_g1.at[x], low_g1.at[x], xy_ssem.at[5, d], xy_rsem.at[5, d], x_devices[d])
-        )
-    for copy in copies:
-        copy.wait()
-
-    copies = []
-    for d in (2, 1, 3):
-        copies.append(
-            start_remote(top_g1, top_all.at[core, x], xy_ssem.at[6, d], xy_rsem.at[6, d], x_devices[d])
-        )
-        copies.append(
-            start_remote(low_g1, low_all.at[core, y], xy_ssem.at[7, d], xy_rsem.at[7, d], y_devices[d])
-        )
-    top_all[core, x] = top_g1[...]
-    low_all[core, y] = low_g1[...]
+            start_remote(z_own, z_all.at[z], z_ssem.at[1, d], z_rsem.at[1, d], z_devices[d])
+        )
+    z_all[z] = z_own[...]
     halo_wait(halo)
     fill_padded(padded2, edge_rows, grad_block, low2h, high2h, left2h, right2h)
 
@@ -418,19 +434,77 @@
         out_grad_ref[b, row] = (misfit[cells] + total).astype(bf16)
 
     run_stencil(padded2, weight, shape, True, finish)
+
+    @pl.when(is_owner)
+    def _():
+        for d in range(1, CHIPS_Z):
+            dw_spread(d).wait_send()
+
+    @pl.when(jnp.logical_not(is_owner))
+    def _():
+        dw_copy.wait_send()
+        pltpu.make_async_remote_copy(
+            src_ref=dw_sum_ref, dst_ref=dw_done, send_sem=dw_ssem.at[0],
+            recv_sem=dw_rsem.at[1, away], device_id=partner, device_id_type=MESH,
+        ).wait_recv()
+
     for copy in copies:
         copy.wait()
-
-    copies = [
-        start_remote(top_all.at[core], top_all.at[core], core_ssem.at[2], core_rsem.at[2], partner),
-        start_remote(low_all.at[core], low_all.at[core], core_ssem.at[3], core_rsem.at[3], partner),
-    ]
+    tiles = z_all[...].reshape(SIDE, SIDE)
+    dw_tile = jnp.concatenate(
+        [dw_done[...], jnp.zeros((DW_PAD - TILE, SIDE), jnp.float32)], axis=0
+    )
+    top_g1[y] = tiles[:SPLIT].astype(jnp.bfloat16)
+    low_g1[x] = jnp.concatenate([tiles[SPLIT:], dw_tile], axis=0).astype(jnp.bfloat16)
+
+    copies = []
+    for d in (2, 1, 3):
+        copies.append(
+            start_remote(top_g1.at[y], top_g1.at[y], xy_ssem.at[4, d], xy_rsem.at[4, d], y_devices[d])
+        )
+        copies.append(
+            start_remote(low_g1.at[x], low_g1.at[x], xy_ssem.at[5, d], xy_rsem.at[5, d], x_devices[d])
+        )
     for copy in copies:
+        copy.wait()
+
+    copies = []
+    for d in (2, 1, 3):
+        copies.append(
+            start_remote(top_g1, top_all.at[core, x], xy_ssem.at[6, d], xy_rsem.at[6, d], x_devices[d])
+        )
+        copies.append(
+            start_remote(low_g1, low_all.at[core, y], xy_ssem.at[7, d], xy_rsem.at[7, d], y_devices[d])
+        )
+    top_all[core, x] = top_g1[...]
+    low_all[core, y] = low_g1[...]
+    core_copies = []
+
+    def to_partner(buffer, slot, k, part):
+        core_copies.append(
+            start_remote(
+                buffer.at[core, slot], buffer.at[core, slot], pair_ssem.at[part, k],
+                pair_rsem.at[part, k], partner,
+            )
+        )
+
+    to_partner(top_all, x, 0, 0)
+    to_partner(low_all, y, 0, 1)
+    for k, d in ((2, 1), (3, 1), (4, 3), (5, 3), (0, 2), (1, 2)):
+        copies[k].wait_recv()
+        if k % 2 == 0:
+            to_partner(top_all, lax.rem(x - d + 4, 4), d, 0)
+        else:
+            to_partner(low_all, lax.rem(y - d + 4, 4), d, 1)
+    for copy in copies:
+        copy.wait_send()
+    for copy in core_copies:
         copy.wait()
     for which, out in enumerate((out_a, out_b)):
         for block in range(BLOCKS):
             bx, by = block // 4, block % 4
-            row, col = SIDE * (block // 8), SIDE * (block % 8)
+            across_blocks = 8 if which == 0 else 2
+            row, col = SIDE * (block // across_blocks), SIDE * (block % across_blocks)
             out[row : row + SPLIT, col : col + SIDE] = top_all[which, bx, by]
             out[row + SPLIT : row + SIDE, col : col + SIDE] = low_all[which, by, bx, : SIDE - SPLIT]
             dw_rows = low_all[which, by, bx, SIDE - SPLIT :].astype(jnp.float32)[:DW_ROWS]
@@ -452,7 +526,7 @@
         step_kernel,
         out_shape=(
             jax.ShapeDtypeStruct(w_in.shape, bf16),
-            jax.ShapeDtypeStruct(w_in.shape, bf16),
+            jax.ShapeDtypeStruct(w_out.shape, bf16),
             jax.ShapeDtypeStruct(dw_shape, f32),
             jax.ShapeDtypeStruct(block.shape, bf16),
         ),
@@ -489,16 +563,22 @@
             pltpu.VMEM(dw_shape[1:], f32),
             pltpu.VMEM((4, 4, SPLIT, SIDE), f32),
             pltpu.VMEM((4, 4, LOWER, SIDE), f32),
-            pltpu.VMEM((4, 4, SPLIT, SIDE), f32),
-            pltpu.VMEM((4, 4, LOWER, SIDE), f32),
+            pltpu.VMEM((4, 4, SPLIT, SIDE), bf16),
+            pltpu.VMEM((4, 4, LOWER, SIDE), bf16),
+            pltpu.VMEM((4, 4, SPLIT, SIDE), bf16),
+            pltpu.VMEM((4, 4, LOWER, SIDE), bf16),
             pltpu.VMEM((4, SPLIT, SIDE), f32),
             pltpu.VMEM((4, LOWER, SIDE), f32),
             pltpu.VMEM((4, SPLIT, SIDE), f32),
             pltpu.VMEM((4, LOWER, SIDE), f32),
-            pltpu.VMEM((CHIPS_Z, 2 * TILE, SIDE), f32),
-            pltpu.VMEM((CHIPS_Z, 2 * TILE, SIDE), f32),
-            pltpu.VMEM((2 * TILE, SIDE), f32),
             pltpu.VMEM((CHIPS_Z, TILE, SIDE), f32),
+            pltpu.VMEM((CHIPS_Z, TILE, SIDE), f32),
+            pltpu.VMEM((TILE, SIDE), f32),
+            pltpu.VMEM((CHIPS_Z, TILE, SIDE), f32),
+            pltpu.VMEM((TILE, SIDE), f32),
+            pltpu.VMEM((CHIPS_Z, TILE, SIDE), f32),
+            pltpu.VMEM((TILE, SIDE), f32),
+            pltpu.VMEM((TILE, SIDE), f32),
             pltpu.VMEM((4, SPLIT, SIDE), bf16),
             pltpu.VMEM((4, LOWER, SIDE), bf16),
             pltpu.VMEM((2, 4, 4, SPLIT, SIDE), bf16),
@@ -516,6 +596,10 @@
             pltpu.SemaphoreType.DMA((lats,)),
             pltpu.SemaphoreType.DMA((lats,)),
             pltpu.SemaphoreType.DMA,
+            pltpu.SemaphoreType.DMA((CHIPS_Z,)),
+            pltpu.SemaphoreType.DMA((2, CHIPS_Z)),
+            pltpu.SemaphoreType.DMA((2, 4)),
+            pltpu.SemaphoreType.DMA((2, 4)),
         ],
         compiler_params=pltpu.CompilerParams(collective_id=0, has_side_effects=True),
     )(block, sent, weight, gain, w_in, w_out, scale)
@@ -537,7 +621,7 @@
     return (
         grad_student,
         sum_in.astype(jnp.float32) / cell_total,
-        sum_out.T.astype(jnp.float32) / cell_total,
+        sum_out.astype(jnp.float32) / cell_total,
         sum_dw / cell_total,
     )
 

time: 92.4 us -> 87.3 us (0.945)
  Pallas kernels: 83.9 us -> 79.3 us
  local copies, waits for them, and re-layouts: 5.19 us -> 3.89 us
    pallas_call x1, Pallas kernels: 83.9 us -> 79.3 us  [whole_step(): pl.pallas_call(step_kernel, out_shape=(jax.ShapeDtypeStruct(w_in.shape, b...]
    unnamed x4 -> x5, local copies, waits for them, and re-layouts: 1.96 us -> 0.66 us
    div x1 -> x2, other arithmetic: 2.44 us -> 3.23 us  [the longest x1 2.19 us: local(): sum_in.astype(jnp.float32) / cell_total]
where the time goes in v5:
time: 87.3 us; the launch traced here: 87.1 us
  Pallas kernels  79.3 us (91%)
  local copies, waits for them, and re-layouts  3.89 us (4%)
  other arithmetic  3.23 us (4%)
    pallas_call x1, Pallas kernels, whole_step(): pl.pallas_call(step_kernel, out_shape=(jax.ShapeDtypeStruct(w_in.shape, b...  79.3 us
    div x1, other arithmetic, local(): sum_in.astype(jnp.float32) / cell_total  2.19 us

profile of v5, /device:TPU:1, one launch (start us, length us, event | category | flops | bytes accessed | tf_op | source)
XLA Modules:
  0.0 87.1 jit_solution(15802435522558776587)
XLA Ops:
  0.6 1.0 %copy.14 = bf16[2,16,4,2,256]{4,3,2,0,1:T(2,128)(2,1)S(1)} copy(bf16[2,16,4,2,256]{4,3,2,1,0:T(2,128)(2,1)} %bitcast.11) | data formatting | bytes 262144 | tf_op jit(solution)/shard_map/reshape | solution.py:613
  1.6 0.7 reshape.21.sent
  2.3 79.3 %shard_map.102 = (bf16[256,1024]{1,0:T(8,128)(2,1)}, bf16[1024,256]{1,0:T(8,128)(2,1)}, f32[2,64,128]{2,1,0:T(8,128)}, bf16[2,4,32,256]{3,2,1,0:T(8,128)(2,1)}) custom-call(bf16[2,4,32,256]{3,2,1,0:T(8,128)(2,1)} %block.1, bf16[16,16,256]{2,1,0:T(8,128)(2,1)} %reshape.21.sent, f32[7,7,256]{2,1,0:T(8,128)} %weight.1, f32[1,256]{1,0:T(1,128)} %bitcast.12, ...), custom_call_target="tpu_custom_call" | custom-call | tf_op jit(solution)/shard_map/pallas_call | solution.py:525
  81.7 0.8 slice_bitcast_fusion
  82.5 0.7 div.29
  83.2 0.0 copy-start
  83.2 2.2 %convert_multiply_fusion.1 = f32[256,1024]{1,0:T(8,128)} fusion(bf16[256,1024]{1,0:T(8,128)(2,1)} %get-tuple-element.9), kind=kLoop, calls=%fused_computation.1 | loop fusion | flops 524288 | bytes 1572864 | tf_op jit(solution)/shard_map/div | solution.py:623
  85.4 0.0 copy-done
  85.4 0.0 copy-start.1
  85.4 1.0 %convert_multiply_fusion = f32[1024,256]{1,0:T(8,128)} fusion(bf16[1024,256]{1,0:T(8,128)(2,1)S(1)} %copy-done), kind=kLoop, calls=%fused_computation | loop fusion | flops 524288 | bytes 1572864 | tf_op jit(solution)/shard_map/div | solution.py:624
  86.4 0.0 copy-done.1
  86.4 0.7 copy.16
  (2 shorter events, 0.0 us)
Async XLA Ops:
  83.2 2.2 %copy-start = (bf16[1024,256]{1,0:T(8,128)(2,1)S(1)}, bf16[1024,256]{1,0:T(8,128)(2,1)}, u32[]{:S(2)}) copy-start(bf16[1024,256]{1,0:T(8,128)(2,1)} %get-tuple-element.10) | copy-start | bytes 1572868
  85.4 1.0 %copy-start.1 = (bf16[2,4,32,256]{3,2,1,0:T(8,128)(2,1)S(1)}, bf16[2,4,32,256]{3,2,1,0:T(8,128)(2,1)}, u32[]{:S(2)}) copy-start(bf16[2,4,32,256]{3,2,1,0:T(8,128)(2,1)} %get-tuple-element.16) | copy-start | bytes 393220

commit v6 on v5

--- a/solution.py
+++ b/solution.py
@@ -163,7 +163,8 @@
 
 
 BLOCKS, SIDE, SPLIT, TILE, DW_ROWS, DW_PAD = 16, 128, 64, 8, 4, 16
-LOWER = SIDE - SPLIT + DW_PAD
+REST = SIDE - SPLIT
+LOWER = REST + DW_PAD
 CHIPS_Z = 16
 CHUNK = 256
 
@@ -179,12 +180,13 @@
     smoothed, unit, hid, slope, misfit, cell_grad, grad_block,
     edges2, low2h, high2h, left2h, right2h, padded2, dw_ref,
     own, other, dw_other, top, low_part, top_b, low_b, top_in1, low_in1, top1, low1, top_in2, low_in2,
-    z_send, z_in, z_own, z_all, dw_send, dw_in, dw_sum_ref, dw_done, top_g1, low_g1, top_all, low_all,
+    z_send, z_in, z_own, z_all, dw_send, dw_in, dw_sum_ref, dw_done, dw_parts, dw_xy, top_g1, low_g1, top_all, low_all,
     core_ssem, core_rsem, xy_ssem, xy_rsem, z_ssem, z_rsem, halo_ssem, halo_rsem,
-    halo2_ssem, halo2_rsem, teach_ssem, teach_rsem, local_sem, dw_ssem, dw_rsem, pair_ssem, pair_rsem,
+    halo2_ssem, halo2_rsem, teach_ssem, teach_rsem, local_sem, dw_ssem, dw_rsem, dw_xy_ssem, dw_xy_rsem, pair_ssem, pair_rsem,
 ):
     f32, bf16 = jnp.float32, jnp.bfloat16
     lats, lons = lax.axis_size("lat"), lax.axis_size("lon")
+    cell_total = block.shape[0] * block.shape[1] * block.shape[2] * lats * lons
     lat, lon = lax.axis_index("lat"), lax.axis_index("lon")
     core = lax.rem(lat, 2)
     z = lax.rem(lon, 2) * 8 + lat // 2
@@ -207,13 +209,15 @@
 
     barrier = pltpu.get_barrier_semaphore()
     friends = [partner] + x_devices[1:] + y_devices[1:] + z_devices[1:]
+    diagonal = [(dx, dy) for dx in range(1, 4) for dy in range(1, 4)]
+    friends = friends + [device(core, z, x_peers[dx], y_peers[dy]) for dx, dy in diagonal]
     lat_peers = [lax.rem(lat + d, lats) for d in range(lats)]
     friends = friends + halo_friends(lat, lon, lats, lons)[:2]
     friends = friends + [{"lat": p, "lon": lon} for p in lat_peers[1:]]
     for friend in friends:
         pl.semaphore_signal(barrier, inc=1, device_id=friend, device_id_type=MESH)
 
-    mine = pltpu.make_async_copy(sent.at[lat], came.at[lat], local_sem)
+    mine = pltpu.make_async_copy(sent.at[:, pl.ds(lat * block.shape[1], block.shape[1])], came.at[lat], local_sem)
     mine.start()
     pack_edges(block, edge_f32, edges)
     pl.semaphore_wait(barrier, len(friends))
@@ -222,7 +226,7 @@
     halo_start(front, low, high, left, right)
     teaching = [
         start_remote(
-            sent.at[lat_peers[d]], came.at[lat], teach_ssem.at[d], teach_rsem.at[d],
+            sent.at[:, pl.ds(lat_peers[d] * block.shape[1], block.shape[1])], came.at[lat], teach_ssem.at[d], teach_rsem.at[d],
             {"lat": lat_peers[d], "lon": lon},
         )
         for d in range(1, lats)
@@ -261,12 +265,13 @@
     for copy in teaching:
         copy.wait()
     for src in range(lats):
-        came_f32[src] = came[src].astype(f32)
+        for n in range(batch * rows):
+            came_f32[src, n] = came[src, n // rows, n % rows].astype(f32)
     part = cols // lats
     for src in range(lats):
         for n in range(batch * rows):
             at = n * cols + src * part
-            target[at : at + part] = came_f32[src, n * part : (n + 1) * part]
+            target[at : at + part] = came_f32[src, n]
     student = jnp.concatenate(
         [block[n // rows, n % rows] for n in range(batch * rows)], axis=0
     ).astype(f32)
@@ -320,20 +325,15 @@
     )
     halo_start(halo, low2h, high2h, left2h, right2h)
     tap_sums(padded, cell_grad, shape, weight.shape[0], dw_ref)
-    copies = core_copies + [
-        start_remote(dw_ref.at[1 - core], dw_other, core_ssem.at[1], core_rsem.at[1], partner),
-    ]
-    for copy in copies:
+    dw_core = start_remote(
+        dw_ref.at[1 - core], dw_other, core_ssem.at[1], core_rsem.at[1], partner
+    )
+    for copy in core_copies:
         copy.wait()
     for block in range(BLOCKS):
         bx, by = block // 4, block % 4
         top[bx, by] = own[core, block, :SPLIT] + other[block, :SPLIT]
-        low_part[by, bx, : SIDE - SPLIT] = own[core, block, SPLIT:] + other[block, SPLIT:]
-        rows = slice(DW_ROWS * block, DW_ROWS * (block + 1))
-        dw_sum = dw_ref[core, rows] + dw_other[rows]
-        low_part[by, bx, SIDE - SPLIT :] = jnp.concatenate(
-            [dw_sum, jnp.zeros((DW_PAD - DW_ROWS, SIDE), jnp.float32)], axis=0
-        )
+        low_part[by, bx] = own[core, block, SPLIT:] + other[block, SPLIT:]
 
     for k in range(4):
         top_b[k] = top[k].astype(bf16)
@@ -346,6 +346,22 @@
         copies.append(
             start_remote(low_b.at[y_peers[d]], low_in1.at[d], xy_ssem.at[1, d], xy_rsem.at[1, d], y_devices[d])
         )
+    dw_core.wait()
+    group = x * 4 + y
+    for slot in range(BLOCKS):
+        lines = slice(DW_ROWS * slot, DW_ROWS * (slot + 1))
+        dw_parts[slot, :DW_ROWS] = dw_ref[core, lines] + dw_other[lines]
+        dw_parts[slot, DW_ROWS:] = jnp.zeros((TILE - DW_ROWS, SIDE), f32)
+    dw_copies = []
+    for k in range(1, BLOCKS):
+        px, py = x_peers[k // 4], y_peers[k % 4]
+        dw_copies.append(
+            start_remote(
+                dw_parts.at[px * 4 + py], dw_xy.at[group], dw_xy_ssem.at[k], dw_xy_rsem.at[k],
+                device(core, z, px, py),
+            )
+        )
+    dw_xy[group] = dw_parts[group]
     for copy in copies:
         copy.wait()
     top1[...] = top[x] + top_in1[1].astype(f32) + top_in1[2].astype(f32) + top_in1[3].astype(f32)
@@ -361,22 +377,13 @@
         copies.append(
             start_remote(low1.at[x_peers[d]], low_in2.at[d], xy_ssem.at[3, d], xy_rsem.at[3, d], x_devices[d])
         )
-    for copy in copies:
-        copy.wait()
-    top2 = top1[y] + top_in2[1] + top_in2[2] + top_in2[3]
-    low2 = low1[x] + low_in2[1] + low_in2[2] + low_in2[3]
-    for tile in range(CHIPS_Z):
-        at = TILE * tile
-        z_send[tile] = top2[at : at + TILE] if at < SPLIT else low2[at - SPLIT : at - SPLIT + TILE]
-    dw_send[...] = low2[SIDE - SPLIT : SIDE - SPLIT + TILE]
-
-    order = [8, 7, 9, 6, 10, 5, 11, 4, 12, 3, 13, 2, 14, 1, 15]
-    copies = []
-    for d in order:
-        copies.append(
-            start_remote(z_send.at[z_peers[d]], z_in.at[z], z_ssem.at[0, d], z_rsem.at[0, d], z_devices[d])
-        )
-    owner = x * 4 + y
+    for copy in dw_copies:
+        copy.wait()
+    dw_line = dw_xy[0]
+    for slot in range(1, BLOCKS):
+        dw_line = dw_line + dw_xy[slot]
+    dw_send[...] = dw_line
+    owner = group
     is_owner = z == owner
     toward = lax.rem(owner - z + CHIPS_Z, CHIPS_Z)
     away = lax.rem(z - owner + CHIPS_Z, CHIPS_Z)
@@ -390,15 +397,22 @@
     def _():
         dw_in[z] = dw_send[...]
 
+    for copy in copies:
+        copy.wait()
+    top2 = top1[y] + top_in2[1] + top_in2[2] + top_in2[3]
+    low2 = low1[x] + low_in2[1] + low_in2[2] + low_in2[3]
+    for tile in range(CHIPS_Z):
+        at = TILE * tile
+        z_send[tile] = top2[at : at + TILE] if at < SPLIT else low2[at - SPLIT : at - SPLIT + TILE]
+
+    order = [8, 7, 9, 6, 10, 5, 11, 4, 12, 3, 13, 2, 14, 1, 15]
+    copies = []
+    for d in order:
+        copies.append(
+            start_remote(z_send.at[z_peers[d]], z_in.at[z], z_ssem.at[0, d], z_rsem.at[0, d], z_devices[d])
+        )
     z_in[z] = z_send[z]
     halo_pass_on(halo)
-    for copy in copies:
-        copy.wait()
-    total = z_in[0]
-    for tile in range(1, CHIPS_Z):
-        total = total + z_in[tile]
-    z_own[...] = total
-
     def dw_spread(d):
         return pltpu.make_async_remote_copy(
             src_ref=dw_sum_ref, dst_ref=dw_done, send_sem=dw_ssem.at[d], recv_sem=dw_rsem.at[1, d],
@@ -420,6 +434,13 @@
             dw_spread(d).start()
         dw_done[...] = dw_total
 
+    for copy in copies:
+        copy.wait()
+    total = z_in[0]
+    for tile in range(1, CHIPS_Z):
+        total = total + z_in[tile]
+    z_own[...] = total
+
     copies = []
     for d in order:
         copies.append(
@@ -507,14 +528,19 @@
             row, col = SIDE * (block // across_blocks), SIDE * (block % across_blocks)
             out[row : row + SPLIT, col : col + SIDE] = top_all[which, bx, by]
             out[row + SPLIT : row + SIDE, col : col + SIDE] = low_all[which, by, bx, : SIDE - SPLIT]
-            dw_rows = low_all[which, by, bx, SIDE - SPLIT :].astype(jnp.float32)[:DW_ROWS]
-            out_dw[which, DW_ROWS * block : DW_ROWS * (block + 1)] = dw_rows
+            p, q = block // 2, DW_ROWS * (block % 2)
+            size = weight.shape[0]
+            if p < size:
+                dw_rows = low_all[which, by, bx, REST:].astype(f32)[: min(DW_ROWS, size - q)]
+                out_dw[p, q : q + dw_rows.shape[0], which * SIDE : (which + 1) * SIDE] = (
+                    dw_rows / cell_total
+                )
 
 
 def whole_step(block, sent, weight, gain, w_in, w_out, scale):
     f32, bf16 = jnp.float32, jnp.bfloat16
     batch, rows, cols, channels = block.shape
-    cells, lats = batch * rows * cols, sent.shape[0]
+    cells, lats = batch * rows * cols, sent.shape[1] // rows
     edge_cells = batch * rows * WIDTH
     vmem = pl.BlockSpec(memory_space=pltpu.VMEM)
     across = pltpu.VMEM((batch, WIDTH, cols, channels), bf16)
@@ -527,7 +553,7 @@
         out_shape=(
             jax.ShapeDtypeStruct(w_in.shape, bf16),
             jax.ShapeDtypeStruct(w_out.shape, bf16),
-            jax.ShapeDtypeStruct(dw_shape, f32),
+            jax.ShapeDtypeStruct(weight.shape, f32),
             jax.ShapeDtypeStruct(block.shape, bf16),
         ),
         in_specs=[vmem] * 7,
@@ -541,8 +567,8 @@
             along,
             pltpu.VMEM((2, 3, edge_cells, channels), f32),
             padded,
-            pltpu.VMEM(sent.shape, bf16),
-            pltpu.VMEM(sent.shape, f32),
+            pltpu.VMEM((lats, batch, rows, sent.shape[2], channels), bf16),
+            pltpu.VMEM((lats, batch * rows, sent.shape[2], channels), f32),
             cell_f32,
             cell_f32,
             cell_f32,
@@ -562,15 +588,15 @@
             pltpu.VMEM((BLOCKS, SIDE, SIDE), f32),
             pltpu.VMEM(dw_shape[1:], f32),
             pltpu.VMEM((4, 4, SPLIT, SIDE), f32),
-            pltpu.VMEM((4, 4, LOWER, SIDE), f32),
+            pltpu.VMEM((4, 4, REST, SIDE), f32),
             pltpu.VMEM((4, 4, SPLIT, SIDE), bf16),
-            pltpu.VMEM((4, 4, LOWER, SIDE), bf16),
+            pltpu.VMEM((4, 4, REST, SIDE), bf16),
             pltpu.VMEM((4, 4, SPLIT, SIDE), bf16),
-            pltpu.VMEM((4, 4, LOWER, SIDE), bf16),
+            pltpu.VMEM((4, 4, REST, SIDE), bf16),
             pltpu.VMEM((4, SPLIT, SIDE), f32),
-            pltpu.VMEM((4, LOWER, SIDE), f32),
+            pltpu.VMEM((4, REST, SIDE), f32),
             pltpu.VMEM((4, SPLIT, SIDE), f32),
-            pltpu.VMEM((4, LOWER, SIDE), f32),
+            pltpu.VMEM((4, REST, SIDE), f32),
             pltpu.VMEM((CHIPS_Z, TILE, SIDE), f32),
             pltpu.VMEM((CHIPS_Z, TILE, SIDE), f32),
             pltpu.VMEM((TILE, SIDE), f32),
@@ -579,6 +605,8 @@
             pltpu.VMEM((CHIPS_Z, TILE, SIDE), f32),
             pltpu.VMEM((TILE, SIDE), f32),
             pltpu.VMEM((TILE, SIDE), f32),
+            pltpu.VMEM((BLOCKS, TILE, SIDE), f32),
+            pltpu.VMEM((BLOCKS, TILE, SIDE), f32),
             pltpu.VMEM((4, SPLIT, SIDE), bf16),
             pltpu.VMEM((4, LOWER, SIDE), bf16),
             pltpu.VMEM((2, 4, 4, SPLIT, SIDE), bf16),
@@ -598,6 +626,8 @@
             pltpu.SemaphoreType.DMA,
             pltpu.SemaphoreType.DMA((CHIPS_Z,)),
             pltpu.SemaphoreType.DMA((2, CHIPS_Z)),
+            pltpu.SemaphoreType.DMA((BLOCKS,)),
+            pltpu.SemaphoreType.DMA((BLOCKS,)),
             pltpu.SemaphoreType.DMA((2, 4)),
             pltpu.SemaphoreType.DMA((2, 4)),
         ],
@@ -607,22 +637,16 @@
 
 def local(student, teacher, dw_weight, norm_gain, w_in, w_out, layer_scale):
     batch_size, tile_rows, tile_cols, channel_count = student.shape
-    kernel_size = dw_weight.shape[0]
     lats = lax.axis_size("lat")
     cell_total = batch_size * tile_rows * lats * tile_cols * lax.axis_size("lon")
-    sent = teacher.reshape(batch_size, lats, -1, teacher.shape[2], channel_count)
-    sent = sent.transpose(1, 0, 2, 3, 4).reshape(lats, -1, channel_count)
     sum_in, sum_out, sum_dw, grad_student = whole_step(
-        student, sent, dw_weight, norm_gain[None], w_in, w_out, layer_scale[None]
-    )
-    sum_dw = sum_dw[:, : kernel_size * TILE].reshape(2, kernel_size, TILE, SIDE)
-    sum_dw = sum_dw[:, :, :kernel_size].transpose(1, 2, 0, 3)
-    sum_dw = sum_dw.reshape(kernel_size, kernel_size, channel_count)
+        student, teacher, dw_weight, norm_gain[None], w_in, w_out, layer_scale[None]
+    )
     return (
         grad_student,
         sum_in.astype(jnp.float32) / cell_total,
         sum_out.astype(jnp.float32) / cell_total,
-        sum_dw / cell_total,
+        sum_dw,
     )
 
 

time: 87.3 us -> 84.3 us (0.966)
  local copies, waits for them, and re-layouts: 3.89 us -> 1.47 us
    reshape x3 -> x0, local copies, waits for them, and re-layouts: 2.54 us -> none  [the longest x1 1 us: local(): teacher.reshape(batch_size, lats, -1, teacher.shape[2], channel_count)]
where the time goes in v6:
time: 84.3 us; the launch traced here: 84.1 us
  Pallas kernels  78.7 us (93%)
  other arithmetic  3.23 us (4%)
  local copies, waits for them, and re-layouts  1.47 us (2%)
    pallas_call x1, Pallas kernels, whole_step(): pl.pallas_call(step_kernel, out_shape=(jax.ShapeDtypeStruct(w_in.shape, b...  78.7 us
    div x1, other arithmetic, local(): sum_in.astype(jnp.float32) / cell_total  2.19 us

profile of v6, /device:TPU:1, one launch (start us, length us, event | category | flops | bytes accessed | tf_op | source)
XLA Modules:
  0.0 84.1 jit_solution(4018621731253596773)
XLA Ops:
  0.6 78.7 %shard_map.102 = (bf16[256,1024]{1,0:T(8,128)(2,1)}, bf16[1024,256]{1,0:T(8,128)(2,1)}, f32[7,7,256]{2,1,0:T(8,128)}, bf16[2,4,32,256]{3,2,1,0:T(8,128)(2,1)}) custom-call(bf16[2,4,32,256]{3,2,1,0:T(8,128)(2,1)} %block.1, bf16[2,64,2,256]{3,2,1,0:T(2,128)(2,1)} %sent.1, f32[7,7,256]{2,1,0:T(8,128)} %weight.1, f32[1,256]{1,0:T(1,128)} %bitcast.2, ...), custom_call_target="tpu_custom_call" | custom-call | tf_op jit(solution)/shard_map/pallas_call | solution.py:551
  79.3 0.0 copy-start
  79.4 2.2 %convert_multiply_fusion.1 = f32[256,1024]{1,0:T(8,128)} fusion(bf16[256,1024]{1,0:T(8,128)(2,1)} %get-tuple-element.9), kind=kLoop, calls=%fused_computation.1 | loop fusion | flops 524288 | bytes 1572864 | tf_op jit(solution)/shard_map/div | solution.py:647
  81.5 0.0 copy-done
  81.5 0.0 copy-start.1
  81.5 1.0 %convert_multiply_fusion = f32[1024,256]{1,0:T(8,128)} fusion(bf16[1024,256]{1,0:T(8,128)(2,1)S(1)} %copy-done), kind=kLoop, calls=%fused_computation | loop fusion | flops 524288 | bytes 1572864 | tf_op jit(solution)/shard_map/div | solution.py:648
  82.6 0.0 copy-done.1
  82.6 0.0 copy-start.2
  82.6 0.7 copy.13
  83.2 0.2 copy-done.2
  83.4 0.6 copy.14
Async XLA Ops:
  79.3 2.2 %copy-start = (bf16[1024,256]{1,0:T(8,128)(2,1)S(1)}, bf16[1024,256]{1,0:T(8,128)(2,1)}, u32[]{:S(2)}) copy-start(bf16[1024,256]{1,0:T(8,128)(2,1)} %get-tuple-element.10) | copy-start | bytes 1572868
  81.5 1.0 %copy-start.1 = (bf16[2,4,32,256]{3,2,1,0:T(8,128)(2,1)S(1)}, bf16[2,4,32,256]{3,2,1,0:T(8,128)(2,1)}, u32[]{:S(2)}) copy-start(bf16[2,4,32,256]{3,2,1,0:T(8,128)(2,1)} %get-tuple-element.16) | copy-start | bytes 393220
  82.6 0.8 %copy-start.2 = (f32[7,7,256]{2,1,0:T(8,128)S(1)}, f32[7,7,256]{2,1,0:T(8,128)}, u32[]{:S(2)}) copy-start(f32[7,7,256]{2,1,0:T(8,128)} %get-tuple-element.19) | copy-start | bytes 150532

commit v7 on v6

--- a/solution.py
+++ b/solution.py
@@ -179,7 +179,7 @@
     edge_f32, edges, low, high, left, right, edge_rows, padded, came, came_f32, target,
     smoothed, unit, hid, slope, misfit, cell_grad, grad_block,
     edges2, low2h, high2h, left2h, right2h, padded2, dw_ref,
-    own, other, dw_other, top, low_part, top_b, low_b, top_in1, low_in1, top1, low1, top_in2, low_in2,
+    own, other, dw_other, top, low_part, top_b, low_b, top_in1, low_in1, top1, low1, top1_b, low1_b, top_in2, low_in2,
     z_send, z_in, z_own, z_all, dw_send, dw_in, dw_sum_ref, dw_done, dw_parts, dw_xy, top_g1, low_g1, top_all, low_all,
     core_ssem, core_rsem, xy_ssem, xy_rsem, z_ssem, z_rsem, halo_ssem, halo_rsem,
     halo2_ssem, halo2_rsem, teach_ssem, teach_rsem, local_sem, dw_ssem, dw_rsem, dw_xy_ssem, dw_xy_rsem, pair_ssem, pair_rsem,
@@ -369,13 +369,15 @@
         low_part[y] + low_in1[1].astype(f32) + low_in1[2].astype(f32) + low_in1[3].astype(f32)
     )
 
+    top1_b[...] = top1[...].astype(bf16)
+    low1_b[...] = low1[...].astype(bf16)
     copies = []
     for d in (2, 1, 3):
         copies.append(
-            start_remote(top1.at[y_peers[d]], top_in2.at[d], xy_ssem.at[2, d], xy_rsem.at[2, d], y_devices[d])
-        )
-        copies.append(
-            start_remote(low1.at[x_peers[d]], low_in2.at[d], xy_ssem.at[3, d], xy_rsem.at[3, d], x_devices[d])
+            start_remote(top1_b.at[y_peers[d]], top_in2.at[d], xy_ssem.at[2, d], xy_rsem.at[2, d], y_devices[d])
+        )
+        copies.append(
+            start_remote(low1_b.at[x_peers[d]], low_in2.at[d], xy_ssem.at[3, d], xy_rsem.at[3, d], x_devices[d])
         )
     for copy in dw_copies:
         copy.wait()
@@ -399,8 +401,8 @@
 
     for copy in copies:
         copy.wait()
-    top2 = top1[y] + top_in2[1] + top_in2[2] + top_in2[3]
-    low2 = low1[x] + low_in2[1] + low_in2[2] + low_in2[3]
+    top2 = top1[y] + top_in2[1].astype(f32) + top_in2[2].astype(f32) + top_in2[3].astype(f32)
+    low2 = low1[x] + low_in2[1].astype(f32) + low_in2[2].astype(f32) + low_in2[3].astype(f32)
     for tile in range(CHIPS_Z):
         at = TILE * tile
         z_send[tile] = top2[at : at + TILE] if at < SPLIT else low2[at - SPLIT : at - SPLIT + TILE]
@@ -439,7 +441,7 @@
     total = z_in[0]
     for tile in range(1, CHIPS_Z):
         total = total + z_in[tile]
-    z_own[...] = total
+    z_own[...] = total.astype(bf16)
 
     copies = []
     for d in order:
@@ -471,7 +473,7 @@
 
     for copy in copies:
         copy.wait()
-    tiles = z_all[...].reshape(SIDE, SIDE)
+    tiles = z_all[...].astype(f32).reshape(SIDE, SIDE)
     dw_tile = jnp.concatenate(
         [dw_done[...], jnp.zeros((DW_PAD - TILE, SIDE), jnp.float32)], axis=0
     )
@@ -595,12 +597,14 @@
             pltpu.VMEM((4, 4, REST, SIDE), bf16),
             pltpu.VMEM((4, SPLIT, SIDE), f32),
             pltpu.VMEM((4, REST, SIDE), f32),
-            pltpu.VMEM((4, SPLIT, SIDE), f32),
-            pltpu.VMEM((4, REST, SIDE), f32),
+            pltpu.VMEM((4, SPLIT, SIDE), bf16),
+            pltpu.VMEM((4, REST, SIDE), bf16),
+            pltpu.VMEM((4, SPLIT, SIDE), bf16),
+            pltpu.VMEM((4, REST, SIDE), bf16),
             pltpu.VMEM((CHIPS_Z, TILE, SIDE), f32),
             pltpu.VMEM((CHIPS_Z, TILE, SIDE), f32),
-            pltpu.VMEM((TILE, SIDE), f32),
-            pltpu.VMEM((CHIPS_Z, TILE, SIDE), f32),
+            pltpu.VMEM((TILE, SIDE), bf16),
+            pltpu.VMEM((CHIPS_Z, TILE, SIDE), bf16),
             pltpu.VMEM((TILE, SIDE), f32),
             pltpu.VMEM((CHIPS_Z, TILE, SIDE), f32),
             pltpu.VMEM((TILE, SIDE), f32),

time: 84.3 us -> 83.3 us (0.988)
  Pallas kernels: 78.7 us -> 77.8 us
    pallas_call x1, Pallas kernels: 78.7 us -> 77.8 us  [whole_step(): pl.pallas_call(step_kernel, out_shape=(jax.ShapeDtypeStruct(w_in.shape, b...]
where the time goes in v7:
time: 83.3 us; the launch traced here: 83.1 us
  Pallas kernels  77.8 us (93%)
  other arithmetic  3.23 us (4%)
  local copies, waits for them, and re-layouts  1.47 us (2%)
    pallas_call x1, Pallas kernels, whole_step(): pl.pallas_call(step_kernel, out_shape=(jax.ShapeDtypeStruct(w_in.shape, b...  77.8 us
    div x1, other arithmetic, local(): sum_in.astype(jnp.float32) / cell_total  2.19 us

profile of v7, /device:TPU:1, one launch (start us, length us, event | category | flops | bytes accessed | tf_op | source)
XLA Modules:
  0.0 83.1 jit_solution(4770424042136617403)
XLA Ops:
  0.6 77.8 %shard_map.102 = (bf16[256,1024]{1,0:T(8,128)(2,1)}, bf16[1024,256]{1,0:T(8,128)(2,1)}, f32[7,7,256]{2,1,0:T(8,128)}, bf16[2,4,32,256]{3,2,1,0:T(8,128)(2,1)}) custom-call(bf16[2,4,32,256]{3,2,1,0:T(8,128)(2,1)} %block.1, bf16[2,64,2,256]{3,2,1,0:T(2,128)(2,1)} %sent.1, f32[7,7,256]{2,1,0:T(8,128)} %weight.1, f32[1,256]{1,0:T(1,128)} %bitcast.2, ...), custom_call_target="tpu_custom_call" | custom-call | tf_op jit(solution)/shard_map/pallas_call | solution.py:553
  78.4 0.0 copy-start
  78.4 2.2 %convert_multiply_fusion.1 = f32[256,1024]{1,0:T(8,128)} fusion(bf16[256,1024]{1,0:T(8,128)(2,1)} %get-tuple-element.9), kind=kLoop, calls=%fused_computation.1 | loop fusion | flops 524288 | bytes 1572864 | tf_op jit(solution)/shard_map/div | solution.py:651
  80.6 0.0 copy-done
  80.6 0.0 copy-start.1
  80.6 1.0 %convert_multiply_fusion = f32[1024,256]{1,0:T(8,128)} fusion(bf16[1024,256]{1,0:T(8,128)(2,1)S(1)} %copy-done), kind=kLoop, calls=%fused_computation | loop fusion | flops 524288 | bytes 1572864 | tf_op jit(solution)/shard_map/div | solution.py:652
  81.6 0.0 copy-done.1
  81.6 0.0 copy-start.2
  81.7 0.7 copy.13
  82.3 0.2 copy-done.2
  82.5 0.6 copy.14
Async XLA Ops:
  78.4 2.2 %copy-start = (bf16[1024,256]{1,0:T(8,128)(2,1)S(1)}, bf16[1024,256]{1,0:T(8,128)(2,1)}, u32[]{:S(2)}) copy-start(bf16[1024,256]{1,0:T(8,128)(2,1)} %get-tuple-element.10) | copy-start | bytes 1572868
  80.6 1.0 %copy-start.1 = (bf16[2,4,32,256]{3,2,1,0:T(8,128)(2,1)S(1)}, bf16[2,4,32,256]{3,2,1,0:T(8,128)(2,1)}, u32[]{:S(2)}) copy-start(bf16[2,4,32,256]{3,2,1,0:T(8,128)(2,1)} %get-tuple-element.16) | copy-start | bytes 393220
  81.6 0.8 %copy-start.2 = (f32[7,7,256]{2,1,0:T(8,128)S(1)}, f32[7,7,256]{2,1,0:T(8,128)}, u32[]{:S(2)}) copy-start(f32[7,7,256]{2,1,0:T(8,128)} %get-tuple-element.19) | copy-start | bytes 150532
